TPU v7x, 256 devices: a whole 4x4x8 slice. The times are simulated.
256 devices in a mesh: wave: 64 (over z, y, core), field: 4 (over x).
Axes of the slice: x: 4, y: 4, z: 8, core: 2. Of those that a mesh axis runs over, the one named last changes fastest.
Arguments:
- spectra: bfloat16 [640, 2, 160, 640], P('wave', None, 'field'), may hold values from -0.15625 to 0.15625
- legendre: bfloat16 [640, 640, 640], P('wave'), may hold values from -0.25 to 0.25
- block_mask: int32 [640, 10, 10], P('wave'), may hold values from 0 to 1, as said below
- wave_slot: int32 [640], replicated, may hold values from 0 to 639, as said below
- lat_order: int32 [1280], replicated, may hold values from 0 to 1279, each once
- level_order: int32 [160], replicated, may hold values from 0 to 159, each once
Outputs:
- grid_fields: bfloat16 [1280, 160, 3072], P('wave', None, 'field')
Inputs may be any that keep to these rules, and one draw needn't show every extreme that they name: `wave_slot`: each wavenumber from 0 to 639 is held by exactly one slot. `block_mask`: a block is 0 where every total wavenumber of its row block lies below the slot's wavenumber; otherwise it is 0 only in the first few latitude blocks from the pole, fewer than half of them.
All inputs are finite; a program needn't handle non-finite values.
Results may differ from a plain program's by a relative error of at most 0.009.
Values may be sent and summed in bfloat16 or wider, within the bound.
A program may use at most 128 MiB of HBM per device.

v0:
```python
import math

import jax
import jax.numpy as jnp
from jax import lax
from jax.sharding import PartitionSpec as P

BLOCK = 64
NLON = 3072


def spread_mask(block_mask):
    grown = jnp.repeat(jnp.repeat(block_mask, BLOCK, axis=1), BLOCK, axis=2)
    return grown > 0


def fourier_tables(wave_slot, lon_index):
    wavenums = jnp.repeat(wave_slot, 2)
    component = jnp.arange(wavenums.shape[0], dtype=jnp.int32) % 2
    phases = wavenums[:, None] * lon_index[None, :] % NLON
    angles = phases.astype(jnp.float32) * jnp.float32(2.0 * math.pi / NLON)
    weight = jnp.where(wavenums == 0, jnp.float32(1.0), jnp.float32(2.0))[:, None]
    entries = jnp.where(
        component[:, None] == 0, weight * jnp.cos(angles), -weight * jnp.sin(angles)
    )
    high_part = entries.astype(jnp.bfloat16)
    low_part = (entries - high_part.astype(jnp.float32)).astype(jnp.bfloat16)
    slots = wave_slot.shape[0]
    return (
        high_part.reshape(slots, 2, lon_index.shape[0]),
        low_part.reshape(slots, 2, lon_index.shape[0]),
    )


def synthesize(coeff_rows, high_part, low_part):
    from_high = jnp.einsum(
        "stcl,scq->tlq", coeff_rows, high_part, preferred_element_type=jnp.float32
    )
    from_low = jnp.einsum("stcl,scq->tlq", coeff_rows, low_part, preferred_element_type=jnp.float32)
    return (from_high + from_low).astype(jnp.bfloat16)


def shards(spectra, legendre, block_mask, wave_slot, lat_order, level_order):
    slot_count = spectra.shape[0]
    spec_len = spectra.shape[3]
    first_slot = lax.axis_index("wave") * slot_count
    my_waves = lax.dynamic_slice_in_dim(wave_slot, first_slot, slot_count)
    degree = jnp.arange(spec_len, dtype=jnp.int32)
    upper_tri = degree[None, :] >= my_waves[:, None]
    even_deg = (degree[None, :] + my_waves[:, None]) % 2 == 0
    zero_bf = jnp.zeros((), jnp.bfloat16)
    even_spec = jnp.where((upper_tri & even_deg)[:, None, None, :], spectra, zero_bf)
    odd_spec = jnp.where((upper_tri & ~even_deg)[:, None, None, :], spectra, zero_bf)
    kept_poly = jnp.where(spread_mask(block_mask), legendre, zero_bf)
    even_sum = jnp.einsum(
        "snj,scln->sjcl", kept_poly, even_spec, preferred_element_type=jnp.float32
    )
    odd_sum = jnp.einsum("snj,scln->sjcl", kept_poly, odd_spec, preferred_element_type=jnp.float32)
    northern = even_sum + odd_sum
    southern = (even_sum - odd_sum)[:, ::-1]
    coeffs = jnp.concatenate([northern, southern], axis=1).astype(jnp.bfloat16)
    coeffs = jnp.take(coeffs, lat_order, axis=1)
    by_latitude = lax.all_to_all(coeffs, "wave", split_axis=1, concat_axis=0, tiled=True)
    high_part, low_part = fourier_tables(wave_slot, jnp.arange(NLON, dtype=jnp.int32))
    grid_local = synthesize(by_latitude, high_part, low_part)
    columns = lax.all_to_all(grid_local, "field", split_axis=2, concat_axis=1, tiled=True)
    return jnp.take(columns, level_order, axis=1)


def solution(mesh):
    placed = (
        P("wave", None, "field", None),
        P("wave", None, None),
        P("wave", None, None),
        P(),
        P(),
        P(),
    )
    return jax.shard_map(
        shards, mesh=mesh, in_specs=placed, out_specs=P("wave", None, "field"), check_vma=False
    )
```

profile of v0, /device:TPU:1, one launch (start us, length us, event | category | flops | bytes accessed | tf_op | source)
XLA Modules:
  0.0 450.5 jit_solution(13107642925932214233)
XLA Ops:
  0.0 0.7 compare_select_fusion
  0.7 0.7 compare_and_fusion
  1.4 0.8 dynamic_slice.3
  2.2 0.1 fusion.31
  2.3 0.0 copy-start.2
  2.3 12.9 %copy.33 = bf16[10,640,640]{1,2,0:T(8,128)(2,1)} copy(bf16[10,640,640]{2,1,0:T(8,128)(2,1)} %param.7) | data formatting | bytes 16384000 | tf_op args[1]
  15.2 0.0 copy-done.2
  15.2 0.2 copy.32
  15.4 0.3 broadcast_in_dim.80
  15.7 0.3 gt.16
  16.0 0.0 copy-start.1
  16.0 7.6 %bitcast_select_fusion = bf16[10,640,640]{1,2,0:T(8,128)(2,1)} fusion(bf16[10,640,640]{1,2,0:T(8,128)(2,1)} %copy.33, pred[10,640,10]{1,2,0:T(8,128)(4,1)S(1)} %gt.16), kind=kLoop, calls=%fused_computation.3 | loop fusion | flops 4096000 | bytes 16448000 | tf_op jit(solution)/shard_map/jit(_where)/select_n | solution.py:54
  23.6 0.0 copy-start
  23.6 0.0 copy-done.1
  23.6 6.5 %fusion.6 = f32[10,640,2,40]{1,3,2,0:T(8,128)S(1)} fusion(bf16[10,640,640]{1,2,0:T(8,128)(2,1)} %bitcast_select_fusion, bf16[10,2,40,640]{3,2,1,0:T(8,128)(2,1)S(1)} %copy-done.1, pred[10,640]{1,0:T(8,128)(4,1)S(1)} %get-tuple-element.7), kind=kOutput, calls=%fused_computation.15 | convolution fusion | flops 655872000 | bytes 11270400 | tf_op jit(solution)/shard_map/snj,scln->sjcl/dot_general | solution.py:58
  30.1 0.0 copy-done
  30.1 3.0 fusion.44
  33.1 0.3 add_convert_fusion
  33.4 2.5 rev.3
  35.9 1.4 pad_maximum_fusion
  37.3 9.8 %copy.36 = bf16[10,1280,2,40]{3,2,1,0:T(2,128)(2,1)} copy(bf16[10,1280,2,40]{1,3,2,0:T(8,128)(2,1)S(1)} %pad_maximum_fusion) | data formatting | bytes 4096000 | tf_op jit(solution)/shard_map/concatenate | solution.py:61
  47.1 46.7 %gather_fusion = bf16[1280,10,2,40]{3,2,1,0:T(2,128)(2,1)} fusion(bf16[10,1280,2,40]{3,2,1,0:T(2,128)(2,1)} %copy.36, s32[2048]{0:T(1024)S(1)} %pad_clamp_fusion), kind=kCustom, calls=%fused_computation | custom fusion | bytes 4101120 | tf_op jit(solution)/shard_map/jit(_take)/gather | solution.py:62
  93.8 11.2 %fusion.45 = bf16[1280,10,2,40]{3,2,1,0:T(2,128)(2,1)} fusion(bf16[1280,10,2,40]{3,2,1,0:T(2,128)(2,1)} %gather_fusion, pred[1280]{0:T(1024)(128)(4,1)S(1)} %compare_and_fusion), kind=kLoop, calls=%fused_computation.65 | loop fusion | flops 1024000 | bytes 4097280
  105.0 0.0 copy-start.3
  105.0 11.3 %reshape.183 = bf16[64,2,8000]{2,1,0:T(2,128)(2,1)} reshape(bf16[1280,10,2,40]{3,2,1,0:T(2,128)(2,1)} %fusion.45) | data formatting | bytes 4096000
  116.4 13.4 %all-to-all-start = ((bf16[64,2,8000]{2,1,0:T(2,128)(2,1)}), bf16[64,2,8000]{2,1,0:T(2,128)(2,1)S(1)}, u32[]{:S(2)}, u32[]{:S(2)}) async-start(bf16[64,2,8000]{2,1,0:T(2,128)(2,1)} %reshape.183), calls=%async_computation | async-start | bytes 4128768 | tf_op jit(solution)/shard_map/all_to_all | solution.py:63
  129.8 0.0 copy-done.3
  129.9 36.1 %fusion.54 = bf16[640,2,3072,1]{2,0,1,3:T(8,128)(2,1)} fusion(f32[640]{0:T(1024)S(1)} %get-tuple-element.6, s32[640]{0:T(1024)S(1)} %copy-done.3, f32[640]{0:T(1024)S(1)} %get-tuple-element.5, pred[640,2]{0,1:T(4,128)(4,1)S(1)} %fusion.34), kind=kLoop, calls=%fused_computation.22.clone.clone.clone.1 | loop fusion | flops 51118080 | bytes 7873280 | tf_op jit(solution)/shard_map/stcl,scq->tlq/dot_general | solution.py:36
  166.0 36.7 %fusion.56 = bf16[640,2,3072,1]{2,0,1,3:T(8,128)(2,1)} fusion(f32[640]{0:T(1024)S(1)} %get-tuple-element.6, s32[640]{0:T(1024)S(1)} %copy-done.3, f32[640]{0:T(1024)S(1)} %get-tuple-element.5, pred[640,2]{0,1:T(4,128)(4,1)S(1)} %fusion.34), kind=kLoop, calls=%fused_computation.19.clone.clone.1 | loop fusion | flops 62914560 | bytes 7873280 | tf_op jit(solution)/shard_map/stcl,scq->tlq/dot_general | solution.py:39
  202.7 0.0 all-to-all-done
  202.7 8.0 %reshape.184 = bf16[1280,10,2,40]{3,2,1,0:T(2,128)(2,1)} reshape(bf16[64,2,8000]{2,1,0:T(2,128)(2,1)S(1)} %all-to-all-done) | data formatting | bytes 4096000
  210.7 6.8 %copy.38 = bf16[64,10,20,2,40]{4,3,2,1,0:T(2,128)(2,1)} copy(bf16[64,10,20,2,40]{4,3,1,2,0:T(2,128)(2,1)} %bitcast.65) | data formatting | bytes 4096000 | tf_op jit(solution)/shard_map/all_to_all | solution.py:63
  217.5 11.9 %copy.39 = bf16[640,20,2,40]{0,3,2,1:T(8,128)(2,1)S(1)} copy(bf16[640,20,2,40]{3,2,1,0:T(2,128)(2,1)} %bitcast.66) | data formatting | bytes 4096000 | tf_op jit(solution)/shard_map/all_to_all | solution.py:63
  229.5 8.9 %fusion.11 = f32[20,40,3072,1]{2,1,3,0:T(8,128)S(1)} fusion(bf16[640,20,2,40]{0,3,2,1:T(8,128)(2,1)S(1)} %copy.39, bf16[640,2,3072,1]{2,0,1,3:T(8,128)(2,1)} %fusion.56), kind=kOutput, calls=%fused_computation.20 | convolution fusion | flops 6291456000 | bytes 19742720 | tf_op jit(solution)/shard_map/stcl,scq->tlq/dot_general | solution.py:39
  238.3 11.4 %fusion.5 = bf16[20,40,3072]{2,1,0:T(8,128)(2,1)} fusion(f32[20,40,3072,1]{2,1,3,0:T(8,128)S(1)} %fusion.11, bf16[640,20,2,40]{0,3,2,1:T(8,128)(2,1)S(1)} %copy.39, bf16[640,2,3072,1]{2,0,1,3:T(8,128)(2,1)} %fusion.54), kind=kOutput, calls=%fused_computation.14 | convolution fusion | flops 6296371200 | bytes 24657920 | tf_op jit(solution)/shard_map/stcl,scq->tlq/dot_general | solution.py:36
  249.8 19.3 %copy.41 = bf16[20,40,3072]{1,0,2:T(8,128)(2,1)} copy(bf16[20,40,3072]{2,1,0:T(8,128)(2,1)} %fusion.5) | data formatting | bytes 9830400 | tf_op jit(solution)/shard_map/convert_element_type | solution.py:40
  269.1 35.7 %reshape.185 = bf16[4,2,307200]{2,1,0:T(2,128)(2,1)} reshape(bf16[3072,20,40]{2,1,0:T(8,128)(2,1)} %bitcast.63) | data formatting | bytes 9830400
  304.8 0.0 copy-start.4
  304.8 5.4 %all-to-all-start.1 = ((bf16[4,2,307200]{2,1,0:T(2,128)(2,1)}), bf16[4,2,307200]{2,1,0:T(2,128)(2,1)}, u32[]{:S(2)}, u32[]{:S(2)}) async-start(bf16[4,2,307200]{2,1,0:T(2,128)(2,1)} %reshape.185), calls=%async_computation.1 | async-start | bytes 9830400 | tf_op jit(solution)/shard_map/all_to_all | solution.py:66
  310.2 0.0 copy-done.4
  310.2 56.3 %all-to-all-done.1 = bf16[4,2,307200]{2,1,0:T(2,128)(2,1)} async-done(((bf16[4,2,307200]{2,1,0:T(2,128)(2,1)}), bf16[4,2,307200]{2,1,0:T(2,128)(2,1)}, u32[]{:S(2)}, u32[]{:S(2)}) %all-to-all-start.1) | async-done | bytes 4915232 | tf_op jit(solution)/shard_map/all_to_all | solution.py:66
  366.5 36.9 %reshape.186 = bf16[3072,20,40]{2,1,0:T(8,128)(2,1)} reshape(bf16[4,2,307200]{2,1,0:T(2,128)(2,1)} %all-to-all-done.1) | data formatting | bytes 9830400
  403.4 20.9 %copy.55 = bf16[20,40,4,768]{3,2,1,0:T(4,128)(2,1)} copy(bf16[20,40,4,768]{1,0,3,2:T(8,128)(2,1)} %bitcast.64) | data formatting | bytes 9830400 | tf_op jit(solution)/shard_map/all_to_all | solution.py:66
  424.3 7.7 %copy.56 = bf16[20,4,40,768]{3,0,2,1:T(8,128)(2,1)} copy(bf16[20,4,40,768]{3,1,2,0:T(4,128)(2,1)} %bitcast.68) | data formatting | bytes 9830400 | tf_op jit(solution)/shard_map/all_to_all | solution.py:66
  432.0 11.3 %gather_fusion.1 = bf16[160,20,768]{2,1,0:T(8,128)(2,1)} fusion(bf16[20,160,768]{2,0,1:T(8,128)(2,1)} %bitcast.67, s32[1024]{0:T(1024)S(1)} %pad_clamp_fusion.1), kind=kCustom, calls=%fused_computation.1 | custom fusion | bytes 9831040 | tf_op jit(solution)/shard_map/jit(_take)/gather | solution.py:67
  443.4 3.3 select_bitcast_fusion
  446.6 3.3 copy.45
  (7 shorter events, 0.1 us)
Async XLA Ops:
  2.3 12.9 %copy-start.2 = (s32[10,10,10]{2,1,0:T(8,128)S(1)}, s32[10,10,10]{2,1,0:T(8,128)}, u32[]{:S(2)}) copy-start(s32[10,10,10]{2,1,0:T(8,128)} %param.8) | copy-start | bytes 12004
  16.0 7.6 %copy-start.1 = (bf16[10,2,40,640]{3,2,1,0:T(8,128)(2,1)S(1)}, bf16[10,2,40,640]{3,2,1,0:T(8,128)(2,1)}, u32[]{:S(2)}) copy-start(bf16[10,2,40,640]{3,2,1,0:T(8,128)(2,1)} %param.6) | copy-start | bytes 3072004
  23.6 6.5 %copy-start = (bf16[10,640,640]{1,2,0:T(8,128)(2,1)S(1)}, bf16[10,640,640]{1,2,0:T(8,128)(2,1)}, u32[]{:S(2)}) copy-start(bf16[10,640,640]{1,2,0:T(8,128)(2,1)} %bitcast_select_fusion) | copy-start | bytes 24576004
  105.0 24.8 %copy-start.3 = (s32[640]{0:T(1024)S(1)}, s32[640]{0:T(1024)}, u32[]{:S(2)}) copy-start(s32[640]{0:T(1024)} %param.9) | copy-start | bytes 7684
  116.4 86.3 %all-to-all-start = ((bf16[64,2,8000]{2,1,0:T(2,128)(2,1)}), bf16[64,2,8000]{2,1,0:T(2,128)(2,1)S(1)}, u32[]{:S(2)}, u32[]{:S(2)}) async-start(bf16[64,2,8000]{2,1,0:T(2,128)(2,1)} %reshape.183), calls=%async_computation | async-start | bytes 4128768 | tf_op jit(solution)/shard_map/all_to_all | solution.py:63
  304.8 5.4 %copy-start.4 = (s32[160]{0:T(256)S(1)}, s32[160]{0:T(256)}, u32[]{:S(2)}) copy-start(s32[160]{0:T(256)} %param.11) | copy-start | bytes 1924
  304.8 61.7 %all-to-all-start.1 = ((bf16[4,2,307200]{2,1,0:T(2,128)(2,1)}), bf16[4,2,307200]{2,1,0:T(2,128)(2,1)}, u32[]{:S(2)}, u32[]{:S(2)}) async-start(bf16[4,2,307200]{2,1,0:T(2,128)(2,1)} %reshape.185), calls=%async_computation.1 | async-start | bytes 9830400 | tf_op jit(solution)/shard_map/all_to_all | solution.py:66
where the time goes:
time: 458 us; the launch traced here: 450 us
  local copies, waits for them, and re-layouts  247 us (54%)
  other arithmetic  98.1 us (21%)
  waiting for transfers between devices  56.3 us (12%)
  matrix products  29.8 us (7%)
  starting transfers between devices  18.8 us (4%)
    unnamed x15, local copies, waits for them, and re-layouts  105 us
    all_to_all x1, waiting for transfers between devices, shards(): lax.all_to_all(grid_local, 'field', split_axis=2, concat_axis=1, tiled=True)  56.3 us
    gather x1, local copies, waits for them, and re-layouts, shards(): coeffs = jnp.take(coeffs, lat_order, axis=1)  46.7 us
    dot_general x1, other arithmetic, synthesize(): jnp.einsum('stcl,scq->tlq', coeff_rows, low_part, preferred_element_type=...  36.7 us
    dot_general x1, other arithmetic, synthesize(): jnp.einsum('stcl,scq->tlq', coeff_rows, high_part, preferred_element_type...  36.1 us
    all_to_all x2, local copies, waits for them, and re-layouts, shards(): lax.all_to_all(grid_local, 'field', split_axis=2, concat_axis=1, tiled=True)  28.6 us
    convert_element_type x1, local copies, waits for them, and re-layouts, synthesize(): return (from_high + from_low).astype(jnp.bfloat16)  19.3 us
    all_to_all x2, local copies, waits for them, and re-layouts, shards(): lax.all_to_all(coeffs, 'wave', split_axis=1, concat_axis=0, tiled=True)  18.7 us
  transfers between devices with their start and end apart: 2, of which 1 were waited for; matrix products, arithmetic and copies ran while one was open for 16% of the time, Pallas kernels for 0%

commit v1 on v0

v1 whole, which is shorter than its diff:
```python
import math

import jax
import jax.numpy as jnp
import numpy as np
from jax import lax
from jax.experimental import pallas as pl
from jax.experimental.pallas import tpu as pltpu
from jax.sharding import PartitionSpec as P

MESH = pl.DeviceIdType.MESH
BF = jnp.bfloat16
F32 = jnp.float32

NLON = 3072
TRUNC = 640
NLAT = 1280
BLOCK = 64
NB = 10
WAVES = 64
FIELDS = 4
SLOTS = 10
LEV = 40
ROWS = 20
HALF = NLON // 2
QUART = NLON // 4

CH = 4
KG = 5
SC = 2 * SLOTS
SCP = 24
TW = 6
NT = 11
KP = NT * 128
BR = 2 * ROWS


def basis_table():
    q = np.arange(QUART)
    parts = []
    for odd in (0, 1):
        m = np.arange(odd, TRUNC, 2)
        ang = 2.0 * math.pi * ((m[:, None] * q[None, :]) % NLON) / NLON
        wt = np.where(m == 0, 1.0, 2.0)[:, None]
        parts += [wt * np.cos(ang), -wt * np.sin(ang)]
    return np.concatenate(parts, axis=0).astype(np.float32).astype(BF)


def regroup_matrix():
    mat = np.zeros((TW * 128, KG * 128), np.float32)
    for j in range(TW):
        for k in range(KG):
            for s in range(SC):
                mat[128 * j + SCP * k + s, 128 * k + SC * j + s] = 1.0
    return mat.astype(BF)


def level_columns():
    f, c, k, g, i = np.meshgrid(np.arange(FIELDS), np.arange(CH), np.arange(KG), np.arange(2), np.arange(4), indexing="ij")
    return (LEV * f + 2 * KG * c + KG * g + k + 1000 * i).reshape(1, -1).astype(np.float32)


def column_of(row_vec):
    return jnp.transpose(jnp.broadcast_to(row_vec, (128, row_vec.shape[1])))


def onehot_rows(ref, row_vec, cols):
    col = column_of(row_vec)
    lane = lax.broadcasted_iota(jnp.int32, col.shape, 1).astype(F32)
    for j in range(cols // 128):
        ref[:, j * 128 : (j + 1) * 128] = (col == lane + float(128 * j)).astype(F32).astype(BF)


def legendre_kernel(ws_ref, spec_ref, leg_ref, mask_ref, vlat_ref, out_ref, kept, z, oht):
    s = pl.program_id(0)
    wavenum = ws_ref[SLOTS * lax.axis_index("wave") + s]

    @pl.when(s == 0)
    def _():
        onehot_rows(oht, vlat_ref[...], NLAT)
        for g in range(2 * CH):
            for k in range(KG):
                at = 128 * g + SCP * k + 16
                z[:, at : at + 8, :] = jnp.zeros((NLAT // 128, 8, 128), F32)
            at = 128 * g + SCP * KG
            z[:, at : at + 8, :] = jnp.zeros((NLAT // 128, 8, 128), F32)

    jb = lax.broadcasted_iota(jnp.int32, (NB, TRUNC), 0) * BLOCK
    jj = lax.broadcasted_iota(jnp.int32, (NB, TRUNC), 1)
    widen = ((jj >= jb) & (jj < jb + BLOCK)).astype(F32)
    lanes = jnp.dot((mask_ref[0] > 0).astype(F32), widen, preferred_element_type=F32).astype(BF)
    for b in range(NB):
        kept[b * BLOCK : (b + 1) * BLOCK, :] = leg_ref[0, b * BLOCK : (b + 1) * BLOCK, :] * lanes[b : b + 1, :]
    degree = lax.broadcasted_iota(jnp.int32, (1, TRUNC), 1)
    upper = degree >= wavenum
    even = ((degree + wavenum) & 1) == 0
    spec = spec_ref[0].reshape(2 * LEV, TRUNC)
    spec_e = spec * jnp.where(upper & even, 1.0, 0.0).astype(BF)
    spec_o = spec * jnp.where(upper & ~even, 1.0, 0.0).astype(BF)
    both = jnp.dot(jnp.concatenate([spec_e, spec_o], axis=0), kept[...], preferred_element_type=F32)
    sums_e, sums_o = both[: 2 * LEV], both[2 * LEV :]
    north, south = sums_e + sums_o, sums_e - sums_o
    for comp in range(2):
        for g in range(2 * CH):
            src = slice(LEV * comp + KG * g, LEV * comp + KG * g + KG)
            dst = pl.ds(128 * g + 2 * s + comp, KG, stride=SCP)
            for t in range(TRUNC // 128):
                z[t, dst, :] = north[src, t * 128 : (t + 1) * 128]
                z[t + TRUNC // 128, dst, :] = south[src, t * 128 : (t + 1) * 128]

    @pl.when(s == SLOTS - 1)
    def _():
        low = lax.broadcasted_iota(jnp.int32, (NLAT // 8, 8, 128), 1) < 4
        for c in range(CH):
            zc = jnp.concatenate([z[t, 256 * c : 256 * (c + 1), :] for t in range(NLAT // 128)], axis=1).astype(BF)
            rows = lax.dot_general(oht[...], zc, (((1,), (1,)), ((), ())), preferred_element_type=F32)
            first = rows[:, :128].reshape(NLAT // 8, 8, 128)
            second = rows[:, 128:].reshape(NLAT // 8, 8, 128)
            tile_a = jnp.where(low, first, pltpu.roll(second, 4, 1))
            tile_b = jnp.where(low, pltpu.roll(first, 4, 1), second)
            tiles = jnp.stack([tile_a, tile_b], axis=1).reshape(WAVES, BR, 128)
            out_ref[c] = tiles.astype(BF)


def legendre_call(wave_slot, spectra, legendre, block_mask, vlat):
    return pl.pallas_call(
        legendre_kernel,
        out_shape=jax.ShapeDtypeStruct((CH, WAVES, BR, 128), BF),
        grid_spec=pltpu.PrefetchScalarGridSpec(
            num_scalar_prefetch=1,
            grid=(SLOTS,),
            in_specs=[
                pl.BlockSpec((1, 2, LEV, TRUNC), lambda s, ws: (s, 0, 0, 0)),
                pl.BlockSpec((1, TRUNC, TRUNC), lambda s, ws: (s, 0, 0)),
                pl.BlockSpec((1, NB, NB), lambda s, ws: (s, 0, 0)),
                pl.BlockSpec((1, NLAT), lambda s, ws: (0, 0)),
            ],
            out_specs=pl.BlockSpec((CH, WAVES, BR, 128), lambda s, ws: (0, 0, 0, 0)),
            scratch_shapes=[
                pltpu.VMEM((TRUNC, TRUNC), BF),
                pltpu.VMEM((NLAT // 128, 2 * CH * 128, 128), F32),
                pltpu.VMEM((NLAT, NLAT), BF),
            ],
        ),
        compiler_params=pltpu.CompilerParams(dimension_semantics=("arbitrary",), vmem_limit_bytes=56 << 20),
        name="legendre",
    )(wave_slot, spectra, legendre, block_mask, vlat)


def build_tables(basis, t_even, t_odd):
    n = TRUNC // 2
    t_even[:, :QUART] = basis[:TRUNC, :]
    t_odd[:, :QUART] = basis[TRUNC:, :]
    row = lax.broadcasted_iota(jnp.int32, (n, 1), 0)
    sign = jnp.where((row & 1) == 0, 1.0, -1.0).astype(F32)
    t_even[:n, QUART:] = (basis[:n, :].astype(F32) * sign).astype(BF)
    t_even[n:, QUART:] = (basis[n : 2 * n, :].astype(F32) * sign).astype(BF)
    t_odd[:n, QUART:] = (basis[3 * n :, :].astype(F32) * sign).astype(BF)
    t_odd[n:, QUART:] = (basis[2 * n : 3 * n, :].astype(F32) * -sign).astype(BF)


def fourier_chunk(recv_c, regroup, lhs, perm, t_even, t_odd, put):
    blocks = jnp.concatenate([recv_c[:, j].reshape(NT * BR, 128) for j in range(TW)], axis=1)
    moved = jnp.dot(blocks, regroup[...], preferred_element_type=F32)
    for k in range(KG):
        for t in range(NT):
            lhs[k * BR : (k + 1) * BR, t * 128 : (t + 1) * 128] = moved[
                t * BR : (t + 1) * BR, k * 128 : (k + 1) * 128
            ].astype(BF)
    ordered = jnp.dot(lhs[...], perm[...], preferred_element_type=F32).astype(BF)
    for h in range(2):
        cols = slice(h * QUART, (h + 1) * QUART)
        g_even = jnp.dot(ordered[:, :TRUNC], t_even[:, cols], preferred_element_type=F32)
        g_odd = jnp.dot(ordered[:, TRUNC:], t_odd[:, cols], preferred_element_type=F32)
        put(h, (g_even + g_odd).astype(BF).reshape(KG, BR, QUART))
        put(h + 2, (g_even - g_odd).astype(BF).reshape(KG, BR, QUART))


def exchange_kernel(
    send_ref, order_ref, basis_ref, regroup_ref, out_ref,
    recv, basis, regroup, perm, t_even, t_odd, lhs, quarters,
    load_sem, send_sem, recv_sem, xsend_sem, xrecv_sem,
):
    w, f = lax.axis_index("wave"), lax.axis_index("field")
    load_b = pltpu.make_async_copy(basis_ref, basis, load_sem.at[0])
    load_b.start()
    load_r = pltpu.make_async_copy(regroup_ref, regroup, load_sem.at[1])
    load_r.start()

    barrier = pltpu.get_barrier_semaphore()

    @pl.loop(1, WAVES)
    def _(d):
        pl.semaphore_signal(barrier, inc=1, device_id=(lax.rem(w + d, WAVES), f), device_id_type=MESH)

    for d in range(1, FIELDS):
        pl.semaphore_signal(barrier, inc=1, device_id=(w, lax.rem(f + d, FIELDS)), device_id_type=MESH)
    pl.semaphore_wait(barrier, WAVES + FIELDS - 2)

    my_tile, my_place = w // TW, lax.rem(w, TW)

    def wave_copy(c, peer):
        return pltpu.make_async_remote_copy(
            src_ref=send_ref.at[c, peer],
            dst_ref=recv.at[c, my_tile, my_place],
            send_sem=send_sem,
            recv_sem=recv_sem.at[c],
            device_id=(peer, f),
            device_id_type=MESH,
        )

    for c in range(CH):
        pltpu.make_async_copy(send_ref.at[c, w], recv.at[c, my_tile, my_place], recv_sem.at[c]).start()

        @pl.loop(1, WAVES // 2)
        def _(d):
            wave_copy(c, lax.rem(w + d, WAVES)).start()
            wave_copy(c, lax.rem(w + WAVES - d, WAVES)).start()

        wave_copy(c, lax.rem(w + WAVES // 2, WAVES)).start()

    for c in range(CH):
        for j in range(WAVES - TW * (NT - 1), TW):
            recv[c, NT - 1, j] = jnp.zeros((BR, 128), BF)
    onehot_rows(perm, order_ref[...], NLAT)
    load_b.wait()
    load_r.wait()
    build_tables(basis, t_even, t_odd)

    for c in range(CH):
        full = send_ref.at[c]
        pltpu.make_async_copy(full, full, recv_sem.at[c]).wait()

        def put(q, value):
            quarters[c, q] = value

        fourier_chunk(recv.at[c], regroup, lhs, perm, t_even, t_odd, put)
        pltpu.make_async_copy(quarters.at[c, f], out_ref.at[f, c], xrecv_sem).start()
        for d in range(1, FIELDS):
            peer = lax.rem(f + d, FIELDS)
            pltpu.make_async_remote_copy(
                src_ref=quarters.at[c, peer],
                dst_ref=out_ref.at[f, c],
                send_sem=xsend_sem,
                recv_sem=xrecv_sem,
                device_id=(w, peer),
                device_id_type=MESH,
            ).start()

    pltpu.make_async_copy(out_ref, out_ref, xrecv_sem).wait()
    sent = quarters.at[:, pl.ds(0, FIELDS - 1)]
    pltpu.make_async_copy(sent, sent, xsend_sem).wait()
    out_blocks = send_ref.at[:, pl.ds(0, WAVES - 1)]
    pltpu.make_async_copy(out_blocks, out_blocks, send_sem).wait()


def exchange_call(send, order):
    anyspace = pl.BlockSpec(memory_space=pl.ANY)
    return pl.pallas_call(
        exchange_kernel,
        out_shape=jax.ShapeDtypeStruct((FIELDS, CH, KG, BR, QUART), BF),
        in_specs=[anyspace, pl.BlockSpec(memory_space=pltpu.VMEM), anyspace, anyspace],
        out_specs=anyspace,
        scratch_shapes=[
            pltpu.VMEM((CH, NT, TW, BR, 128), BF),
            pltpu.VMEM((2 * TRUNC, QUART), BF),
            pltpu.VMEM((TW * 128, KG * 128), BF),
            pltpu.VMEM((KP, NLAT), BF),
            pltpu.VMEM((TRUNC, HALF), BF),
            pltpu.VMEM((TRUNC, HALF), BF),
            pltpu.VMEM((KG * BR, KP), BF),
            pltpu.VMEM((CH, FIELDS, KG, BR, QUART), BF),
            pltpu.SemaphoreType.DMA((2,)),
            pltpu.SemaphoreType.DMA,
            pltpu.SemaphoreType.DMA((CH,)),
            pltpu.SemaphoreType.DMA,
            pltpu.SemaphoreType.DMA,
        ],
        compiler_params=pltpu.CompilerParams(collective_id=0, has_side_effects=True, vmem_limit_bytes=56 << 20),
        name="exchange",
    )(send, order, jnp.asarray(basis_table()), jnp.asarray(regroup_matrix()))


def level_kernel(grid_ref, rowkey_ref, colkey_ref, out_ref, pick):
    @pl.when(pl.program_id(0) == 0)
    def _():
        col = column_of(rowkey_ref[...])
        for j in range(LEV * FIELDS * 4 // 128):
            pick[:, j * 128 : (j + 1) * 128] = (
                (col == colkey_ref[:, j * 128 : (j + 1) * 128]).astype(F32).astype(BF)
            )

    rows = grid_ref[...].reshape(FIELDS * CH * KG * 8, QUART)
    out = jnp.dot(pick[...], rows, preferred_element_type=F32)
    out_ref[...] = out.astype(BF).reshape(4, FIELDS * LEV, QUART)


def level_call(grid, rowkey):
    n = FIELDS * LEV * 4
    return pl.pallas_call(
        level_kernel,
        out_shape=jax.ShapeDtypeStruct((ROWS, FIELDS * LEV, QUART), BF),
        grid=(ROWS // 4,),
        in_specs=[
            pl.BlockSpec((FIELDS, CH, KG, 8, QUART), lambda i: (0, 0, 0, i, 0)),
            pl.BlockSpec((1, n), lambda i: (0, 0)),
            pl.BlockSpec((1, n), lambda i: (0, 0)),
        ],
        out_specs=pl.BlockSpec((4, FIELDS * LEV, QUART), lambda i: (i, 0, 0)),
        scratch_shapes=[pltpu.VMEM((n, n), BF)],
        compiler_params=pltpu.CompilerParams(dimension_semantics=("arbitrary",), vmem_limit_bytes=40 << 20),
        name="levels",
    )(grid, rowkey, jnp.asarray(level_columns()))


def index_rows(wave_slot, lat_order, level_order):
    vlat = jnp.where(lat_order < TRUNC, lat_order, NLAT + TRUNC - 1 - lat_order).astype(F32).reshape(1, NLAT)
    comp = jnp.arange(2, dtype=jnp.int32)
    place = TRUNC * (wave_slot & 1)[:, None] + (TRUNC // 2) * comp[None, :] + (wave_slot >> 1)[:, None]
    place = place.reshape(WAVES, SC).astype(F32)
    place = jnp.pad(place, ((0, NT * TW - WAVES), (0, 0)), constant_values=-1.0).reshape(NT, TW * SC)
    order = jnp.pad(place, ((0, 0), (0, 128 - TW * SC)), constant_values=-1.0).reshape(1, KP)
    rowkey = (level_order[None, :] + 1000 * jnp.arange(4, dtype=jnp.int32)[:, None]).astype(F32).reshape(1, -1)
    return vlat, order, rowkey


def shards(spectra, legendre, block_mask, wave_slot, lat_order, level_order):
    vlat, order, rowkey = index_rows(wave_slot, lat_order, level_order)
    send = legendre_call(wave_slot, spectra, legendre, block_mask, vlat)
    grid = exchange_call(send, order)
    return level_call(grid, rowkey)


def solution(mesh):
    placed = (
        P("wave", None, "field", None),
        P("wave", None, None),
        P("wave", None, None),
        P(),
        P(),
        P(),
    )
    return jax.shard_map(
        shards, mesh=mesh, in_specs=placed, out_specs=P("wave", None, "field"), check_vma=False
    )
```

time: 458 us -> 119 us (0.26); the launches traced: 450 us -> 117 us
  local copies, waits for them, and re-layouts: 247 us -> 4.41 us
  Pallas kernels: 0 us -> 110 us
  other arithmetic: 98.1 us -> 2.23 us
  waiting for transfers between devices: 56.3 us -> 0 us
  matrix products: 29.8 us -> 0 us
  starting transfers between devices: 18.8 us -> 0 us
    pallas_call x0 -> x3, Pallas kernels: none -> 110 us  [the longest x1 87.6 us: exchange_call(): pl.pallas_call(exchange_kernel, out_shape=jax.ShapeDtypeStruct((FIELDS, C...]
    unnamed x15 -> x7, local copies, waits for them, and re-layouts: 105 us -> 3.1 us
    dot_general x2 -> x0, other arithmetic: 72.8 us -> none  [the longest x1 36.7 us: synthesize(): jnp.einsum('stcl,scq->tlq', coeff_rows, low_part, preferred_element_type=...]
    gather x2 -> x0, local copies, waits for them, and re-layouts: 58.1 us -> none  [the longest x1 46.7 us: shards(): coeffs = jnp.take(coeffs, lat_order, axis=1)]
    all_to_all x2 -> x0, waiting for transfers between devices: 56.3 us -> none  [the longest x1 56.3 us: shards(): lax.all_to_all(grid_local, 'field', split_axis=2, concat_axis=1, tiled=True)]
    all_to_all x4 -> x0, local copies, waits for them, and re-layouts: 47.3 us -> none  [the longest x2 28.6 us: shards(): lax.all_to_all(grid_local, 'field', split_axis=2, concat_axis=1, tiled=True)]
    dot_general x4 -> x0, matrix products: 29.8 us -> none  [the longest x1 11.4 us: synthesize(): jnp.einsum('stcl,scq->tlq', coeff_rows, high_part, preferred_element_type...]
    convert_element_type x1, local copies, waits for them, and re-layouts: 19.3 us -> 0.09 us  [index_rows(): (level_order[None, :] + 1000 * jnp.arange(4, dtype=jnp.int32)[:, None]).a...]
  transfers between devices with their start and end apart: 2 -> 0, of which waited for: 1 -> 0; matrix products, arithmetic and copies ran while one was open for 16% -> 0% of each run, Pallas kernels for 0% -> 0%
where the time goes in v1:
time: 119 us; the launch traced here: 117 us
  Pallas kernels  110 us (92%)
  local copies, waits for them, and re-layouts  4.41 us (4%)
  other arithmetic  2.23 us (2%)
    pallas_call x1, Pallas kernels, exchange_call(): pl.pallas_call(exchange_kernel, out_shape=jax.ShapeDtypeStruct((FIELDS, C...  87.6 us
    pallas_call x1, Pallas kernels, legendre_call(): pl.pallas_call(legendre_kernel, out_shape=jax.ShapeDtypeStruct((CH, WAVES...  16.5 us
    pallas_call x1, Pallas kernels, level_call(): pl.pallas_call(level_kernel, out_shape=jax.ShapeDtypeStruct((ROWS, FIELDS...  6.24 us
    unnamed x7, local copies, waits for them, and re-layouts  3.1 us

profile of v1, /device:TPU:1, one launch (start us, length us, event | category | flops | bytes accessed | tf_op | source)
XLA Modules:
  0.0 117.1 jit_solution(14199021009774459405)
XLA Ops:
  0.0 0.7 add_convert_fusion.1
  0.8 0.1 convert_element_type.22.rowkey_ref
  0.8 0.1 add.64
  0.9 0.7 fusion
  1.6 0.6 reshape.58.vlat_ref
  2.2 0.7 and_multiply_fusion
  2.9 0.1 add.60
  3.1 0.1 copy.10
  3.2 0.1 add.67
  3.3 0.1 copy.11
  3.4 0.1 add_convert_fusion
  3.5 0.1 copy.13
  3.6 0.1 reshape.59
  3.7 0.6 copy.16
  4.3 16.5 %legendre.1.send_ref = bf16[4,64,40,128]{3,2,1,0:T(8,128)(2,1)} custom-call(s32[640]{0:T(1024)} %ws_ref.1, bf16[10,2,40,640]{3,2,1,0:T(8,128)(2,1)} %spec_ref.1, bf16[10,640,640]{2,1,0:T(8,128)(2,1)} %leg_ref.1, s32[10,10,10]{2,1,0:T(8,128)} %mask_ref.1, f32[1,1280]{1,0:T(1,128)} %reshape.58.vlat_ref), custom_call_target="tpu_custom_call" | custom-call | tf_op jit(solution)/shard_map/legendre/pallas_call | solution.py:126
  20.8 0.0 copy-start.1
  20.8 87.6 %exchange.1.grid_ref = bf16[4,4,5,40,768]{4,3,2,1,0:T(8,128)(2,1)} custom-call(bf16[4,64,40,128]{3,2,1,0:T(8,128)(2,1)} %legendre.1.send_ref, f32[1,1408]{1,0:T(1,128)} %bitcast.10, bf16[1280,768]{1,0:T(8,128)(2,1)} %constant.8.clone.basis_ref, bf16[768,640]{1,0:T(8,128)(2,1)} %constant.20.clone.regroup_ref), custom_call_target="tpu_custom_call" | custom-call | tf_op jit(solution)/shard_map/exchange/pallas_call | solution.py:259
  108.4 0.0 copy-done.1
  108.4 0.0 copy-start
  108.4 2.4 %copy-done = bf16[4,4,5,40,768]{4,3,2,1,0:T(8,128)(2,1)S(1)} copy-done((bf16[4,4,5,40,768]{4,3,2,1,0:T(8,128)(2,1)S(1)}, bf16[4,4,5,40,768]{4,3,2,1,0:T(8,128)(2,1)}, u32[]{:S(2)}) %copy-start) | copy-done | bytes 4915224
  110.8 6.2 %levels.1 = bf16[20,160,768]{2,1,0:T(8,128)(2,1)} custom-call(bf16[4,4,5,40,768]{4,3,2,1,0:T(8,128)(2,1)S(1)} %copy-done, f32[1,640]{1,0:T(1,128)S(1)} %convert_element_type.22.rowkey_ref, f32[1,640]{1,0:T(1,128)S(1)} %copy-done.1), custom_call_target="tpu_custom_call" | custom-call | tf_op jit(solution)/shard_map/levels/pallas_call | solution.py:300
  (9 shorter events, 0.1 us)
Async XLA Ops:
  20.8 87.7 %copy-start.1 = (f32[1,640]{1,0:T(1,128)S(1)}, f32[1,640]{1,0:T(1,128)}, u32[]{:S(2)}) copy-start(f32[1,640]{1,0:T(1,128)} %constant.21.clone.colkey_ref) | copy-start | bytes 7684
  108.4 2.4 %copy-start = (bf16[4,4,5,40,768]{4,3,2,1,0:T(8,128)(2,1)S(1)}, bf16[4,4,5,40,768]{4,3,2,1,0:T(8,128)(2,1)}, u32[]{:S(2)}) copy-start(bf16[4,4,5,40,768]{4,3,2,1,0:T(8,128)(2,1)} %exchange.1.grid_ref) | copy-start | bytes 14745604

commit v2 on v0

v2 whole, which is shorter than its diff:
```python
import math

import jax
import jax.numpy as jnp
import numpy as np
from jax import lax
from jax.experimental import pallas as pl
from jax.experimental.pallas import tpu as pltpu
from jax.sharding import PartitionSpec as P

MESH = pl.DeviceIdType.MESH
BF = jnp.bfloat16
F32 = jnp.float32

NLON = 3072
TRUNC = 640
NLAT = 1280
BLOCK = 64
NB = 10
WAVES = 64
FIELDS = 4
SLOTS = 10
LEV = 40
ROWS = 20
HALF = NLON // 2
QUART = NLON // 4

CH = 5
RW = ROWS // CH
KG = 6
NG = 7
SC = 2 * SLOTS
TW = 6
NT = 11
KP = NT * 128
MR = RW * LEV
CUT = 3
LT = NLAT // 128
PIECES = [(0, 0, CUT), (0, CUT, NG)] + [(c, 0, NG) for c in range(1, CH)]


def row_runs():
    runs, at = [], 0
    for low, high in ((0, CUT), (CUT, NG)):
        for k in range(KG):
            top = min(high, (LEV - k + KG - 1) // KG)
            runs.append((k, low, top, at))
            at += RW * (top - low)
    return runs


def basis_table():
    q = np.arange(QUART)
    parts = []
    for odd in (0, 1):
        m = np.arange(odd, TRUNC, 2)
        ang = 2.0 * math.pi * ((m[:, None] * q[None, :]) % NLON) / NLON
        wt = np.where(m == 0, 1.0, 2.0)[:, None]
        parts += [wt * np.cos(ang), -wt * np.sin(ang)]
    return np.concatenate(parts, axis=0).astype(np.float32).astype(BF)


def key_rows():
    keys = np.full((2, TW * 128), -1.0, np.float32)
    for j in range(TW):
        for k in range(KG):
            for s in range(SC):
                keys[0, 128 * j + SC * k + s] = 128 * k + 60 * (s // SLOTS) + SLOTS * j + s % SLOTS
    for f in range(FIELDS):
        for k, low, top, at in row_runs():
            for g in range(low, top):
                for i in range(RW):
                    keys[1, MR * f + at + RW * (g - low) + i] = LEV * f + KG * g + k + 1000 * i
    return keys


def column_of(row_vec):
    return jnp.transpose(jnp.broadcast_to(row_vec, (128, row_vec.shape[1])))


def columns_of(rows):
    return jnp.concatenate([column_of(rows[t : t + 1, :]) for t in range(rows.shape[0])], axis=0)


def fill_onehot(ref, col, cols):
    lane = lax.broadcasted_iota(jnp.int32, col.shape, 1).astype(F32)
    for j in range(cols // 128):
        ref[:, j * 128 : (j + 1) * 128] = (col == lane + float(128 * j)).astype(F32).astype(BF)


def clear_pads(z):
    for g in range(NG):
        z[:, 128 * g + SC * KG : 128 * (g + 1), :] = jnp.zeros((LT, 128 - SC * KG, 128), F32)
    first = 128 * (NG - 1) + SC * (LEV - KG * (NG - 1))
    z[:, first : 128 * NG, :] = jnp.zeros((LT, 128 * NG - first, 128), F32)


def legendre_slot(s, wavenum, spec, leg, mask, kept, z):
    jb = lax.broadcasted_iota(jnp.int32, (NB, TRUNC), 0) * BLOCK
    jj = lax.broadcasted_iota(jnp.int32, (NB, TRUNC), 1)
    widen = ((jj >= jb) & (jj < jb + BLOCK)).astype(F32)
    lanes = jnp.dot((mask[s] > 0).astype(F32), widen, preferred_element_type=F32).astype(BF)
    for b in range(NB):
        kept[b * BLOCK : (b + 1) * BLOCK, :] = leg[s, b * BLOCK : (b + 1) * BLOCK, :] * lanes[b : b + 1, :]
    degree = lax.broadcasted_iota(jnp.int32, (1, TRUNC), 1)
    upper = degree >= wavenum
    even = ((degree + wavenum) & 1) == 0
    rows = spec[s].reshape(2 * LEV, TRUNC)
    rows_e = rows * jnp.where(upper & even, 1.0, 0.0).astype(BF)
    rows_o = rows * jnp.where(upper & ~even, 1.0, 0.0).astype(BF)
    both = jnp.dot(jnp.concatenate([rows_e, rows_o], axis=0), kept[...], preferred_element_type=F32)
    sums_e, sums_o = both[: 2 * LEV], both[2 * LEV :]
    north, south = sums_e + sums_o, sums_e - sums_o
    for comp in range(2):
        for g in range(NG):
            n = min(KG, LEV - KG * g)
            src = slice(LEV * comp + KG * g, LEV * comp + KG * g + n)
            dst = pl.ds(128 * g + SLOTS * comp + s, n, stride=SC)
            for t in range(TRUNC // 128):
                z[t, dst, :] = north[src, t * 128 : (t + 1) * 128]
                z[t + TRUNC // 128, dst, :] = south[src, t * 128 : (t + 1) * 128]


def pack_chunk(c, vcol, oht, zb, send):
    fill_onehot(oht, vcol[pl.ds(c, NLAT // CH, stride=CH), :], NLAT)
    rows = lax.dot_general(oht[...], zb[...], (((1,), (1,)), ((), ())), preferred_element_type=F32)
    for g in range(NG):
        send[c, :, g] = rows[:, 128 * g : 128 * (g + 1)].reshape(WAVES, RW, 128).astype(BF)


def fill_order(slots, keycol, perm):
    m = columns_of(slots[...])
    half = jnp.floor(m * 0.5)
    key = TRUNC * (m - 2.0 * half) + half
    keycol[...] = jnp.full((KP, 128), -1.0, F32)
    for t in range(NT):
        n = min(TW * SLOTS, TRUNC - TW * SLOTS * t)
        part = key[TW * SLOTS * t : TW * SLOTS * t + n]
        for comp in range(2):
            keycol[128 * t + 60 * comp : 128 * t + 60 * comp + n, :] = part + float(TRUNC // 2 * comp)
    fill_onehot(perm, keycol[...], NLAT)


def fill_tables(basis, t_even, t_odd):
    n = TRUNC // 2
    t_even[:, :QUART] = basis[:TRUNC, :]
    t_odd[:, :QUART] = basis[TRUNC:, :]
    row = lax.broadcasted_iota(jnp.int32, (n, 1), 0)
    sign = jnp.where((row & 1) == 0, 1.0, -1.0).astype(F32)
    t_even[:n, QUART:] = (basis[:n, :].astype(F32) * sign).astype(BF)
    t_even[n:, QUART:] = (basis[n : 2 * n, :].astype(F32) * sign).astype(BF)
    t_odd[:n, QUART:] = (basis[3 * n :, :].astype(F32) * sign).astype(BF)
    t_odd[n:, QUART:] = (basis[2 * n : 3 * n, :].astype(F32) * -sign).astype(BF)


def fourier_piece(c, low, high, recv, regroup, lhs, perm, t_even, t_odd, quarters):
    ng = high - low
    blocks = jnp.concatenate(
        [recv[c, :, j, low:high].reshape(NT * ng * RW, 128) for j in range(TW)], axis=1
    )
    moved = jnp.dot(blocks, regroup[...], preferred_element_type=F32)
    runs = [r for r in row_runs() if low <= r[1] and r[1] < high]
    first = runs[0][3]
    last = first
    for k, start, top, at in runs:
        n = RW * (top - start)
        last = at + n
        for t in range(NT):
            src = t * ng * RW + RW * (start - low)
            lhs[at : at + n, t * 128 : (t + 1) * 128] = moved[src : src + n, k * 128 : (k + 1) * 128]
    ordered = jnp.dot(lhs[first:last, :].astype(BF), perm[...], preferred_element_type=F32).astype(BF)
    for h in range(2):
        cols = slice(h * QUART, (h + 1) * QUART)
        g_even = jnp.dot(ordered[:, :TRUNC], t_even[:, cols], preferred_element_type=F32)
        g_odd = jnp.dot(ordered[:, TRUNC:], t_odd[:, cols], preferred_element_type=F32)
        quarters[c, h, first:last, :] = (g_even + g_odd).astype(BF)
        quarters[c, h + 2, first:last, :] = (g_even - g_odd).astype(BF)
    return first, last - first


def fill_levels(levels, colkey, pick):
    col = columns_of(levels[...])[: FIELDS * LEV]
    for i in range(RW):
        for j in range(FIELDS * MR // 128):
            hit = col + float(1000 * i) == colkey[1:2, j * 128 : (j + 1) * 128]
            pick[FIELDS * LEV * i : FIELDS * LEV * (i + 1), j * 128 : (j + 1) * 128] = hit.astype(F32).astype(BF)


def transform_kernel(
    ws_ref, spec_ref, leg_ref, mask_ref, slots_ref, lats_ref, levels_ref, keys_ref, basis_ref, out_ref,
    spec, leg, kept, z, zb, vcol, oht, send, recv, basis, regroup, keycol, perm, t_even, t_odd, lhs,
    quarters, xrecv, pick, stage,
    leg_sem, load_sem, send_sem, recv_sem, xsend_sem, xrecv_sem, out_sem,
):
    w, f = lax.axis_index("wave"), lax.axis_index("field")
    loads = [pltpu.make_async_copy(spec_ref, spec, load_sem.at[0]), pltpu.make_async_copy(basis_ref, basis, load_sem.at[1])]
    slot_loads = [pltpu.make_async_copy(leg_ref.at[s], leg.at[s], leg_sem.at[s]) for s in range(SLOTS)]
    loads[0].start()
    for load in slot_loads:
        load.start()
    loads[1].start()

    barrier = pltpu.get_barrier_semaphore()

    @pl.loop(1, WAVES)
    def _(d):
        pl.semaphore_signal(barrier, inc=1, device_id=(lax.rem(w + d, WAVES), f), device_id_type=MESH)

    for d in range(1, FIELDS):
        pl.semaphore_signal(barrier, inc=1, device_id=(w, lax.rem(f + d, FIELDS)), device_id_type=MESH)

    lat = columns_of(lats_ref[...])
    vcol[...] = jnp.where(lat < TRUNC, lat, (NLAT + TRUNC - 1) - lat)
    clear_pads(z)
    loads[0].wait()

    @pl.loop(0, SLOTS)
    def _(s):
        pltpu.make_async_copy(leg_ref.at[s], leg.at[s], leg_sem.at[s]).wait()
        legendre_slot(s, ws_ref[SLOTS * w + s], spec, leg, mask_ref, kept, z)

    zb[...] = jnp.concatenate([z[t] for t in range(LT)], axis=1).astype(BF)

    my_tile, my_place = w // TW, lax.rem(w, TW)

    def wave_copy(p, peer):
        c, low, high = PIECES[p]
        return pltpu.make_async_remote_copy(
            src_ref=send.at[c, peer, pl.ds(low, high - low)],
            dst_ref=recv.at[c, my_tile, my_place, pl.ds(low, high - low)],
            send_sem=send_sem,
            recv_sem=recv_sem.at[p],
            device_id=(peer, f),
            device_id_type=MESH,
        )

    for p, (c, low, high) in enumerate(PIECES):
        if low == 0:
            pack_chunk(c, vcol, oht, zb, send)
        if p == 0:
            pl.semaphore_wait(barrier, WAVES + FIELDS - 2)
        span = pl.ds(low, high - low)
        pltpu.make_async_copy(send.at[c, w, span], recv.at[c, my_tile, my_place, span], recv_sem.at[p]).start()

        @pl.loop(1, WAVES // 2)
        def _(d):
            wave_copy(p, lax.rem(w + d, WAVES)).start()
            wave_copy(p, lax.rem(w + WAVES - d, WAVES)).start()

        wave_copy(p, lax.rem(w + WAVES // 2, WAVES)).start()

    for c in range(CH):
        for j in range(WAVES - TW * (NT - 1), TW):
            recv[c, NT - 1, j] = jnp.zeros((NG, RW, 128), BF)
    fill_onehot(regroup, column_of(keys_ref[0:1, :]), KG * 128)
    fill_order(slots_ref, keycol, perm)
    loads[1].wait()
    fill_tables(basis, t_even, t_odd)
    fill_levels(levels_ref, keys_ref, pick)

    def out_copies(c):
        return [pltpu.make_async_copy(stage.at[c % 2, i], out_ref.at[CH * i + c], out_sem.at[c % 2, i]) for i in range(RW)]

    def finish_chunk(c):
        pltpu.make_async_copy(xrecv.at[c], xrecv.at[c], xrecv_sem.at[c]).wait()
        rows = xrecv[c].reshape(FIELDS * MR, QUART)
        if c >= 2:
            for copy in out_copies(c - 2):
                copy.wait()
        values = jnp.dot(pick[...], rows, preferred_element_type=F32).astype(BF)
        stage[c % 2] = values.reshape(RW, FIELDS * LEV, QUART)
        for copy in out_copies(c):
            copy.start()

    for p, (c, low, high) in enumerate(PIECES):
        landed = send.at[c, :, pl.ds(low, high - low)]
        pltpu.make_async_copy(landed, landed, recv_sem.at[p]).wait()
        first, count = fourier_piece(c, low, high, recv, regroup, lhs, perm, t_even, t_odd, quarters)
        part = pl.ds(first, count)
        pltpu.make_async_copy(quarters.at[c, f, part], xrecv.at[c, f, part], xrecv_sem.at[c]).start()
        for d in range(1, FIELDS):
            peer = lax.rem(f + d, FIELDS)
            pltpu.make_async_remote_copy(
                src_ref=quarters.at[c, peer, part],
                dst_ref=xrecv.at[c, f, part],
                send_sem=xsend_sem,
                recv_sem=xrecv_sem.at[c],
                device_id=(w, peer),
                device_id_type=MESH,
            ).start()
        if high == NG and c >= 1:
            finish_chunk(c - 1)
    finish_chunk(CH - 1)

    for c in (CH - 2, CH - 1):
        for copy in out_copies(c):
            copy.wait()
    sent = quarters.at[:, pl.ds(0, FIELDS - 1)]
    pltpu.make_async_copy(sent, sent, xsend_sem).wait()
    left = send.at[:, pl.ds(0, WAVES - 1)]
    pltpu.make_async_copy(left, left, send_sem).wait()


def shards(spectra, legendre, block_mask, wave_slot, lat_order, level_order):
    slots = wave_slot.astype(F32).reshape(TRUNC // 128, 128)
    lats = lat_order.astype(F32).reshape(LT, 128)
    levels = jnp.pad(level_order, (0, 256 - FIELDS * LEV)).astype(F32).reshape(2, 128)
    anyspace = pl.BlockSpec(memory_space=pl.ANY)
    vmem = pl.BlockSpec(memory_space=pltpu.VMEM)
    return pl.pallas_call(
        transform_kernel,
        out_shape=jax.ShapeDtypeStruct((ROWS, FIELDS * LEV, QUART), BF),
        in_specs=[pl.BlockSpec(memory_space=pltpu.SMEM), anyspace, anyspace, vmem, vmem, vmem, vmem, vmem, anyspace],
        out_specs=anyspace,
        scratch_shapes=[
            pltpu.VMEM((SLOTS, 2, LEV, TRUNC), BF),
            pltpu.VMEM((SLOTS, TRUNC, TRUNC), BF),
            pltpu.VMEM((TRUNC, TRUNC), BF),
            pltpu.VMEM((LT, NG * 128, 128), F32),
            pltpu.VMEM((NG * 128, NLAT), BF),
            pltpu.VMEM((NLAT, 128), F32),
            pltpu.VMEM((NLAT // CH, NLAT), BF),
            pltpu.VMEM((CH, WAVES, NG, RW, 128), BF),
            pltpu.VMEM((CH, NT, TW, NG, RW, 128), BF),
            pltpu.VMEM((2 * TRUNC, QUART), BF),
            pltpu.VMEM((TW * 128, KG * 128), BF),
            pltpu.VMEM((KP, 128), F32),
            pltpu.VMEM((KP, NLAT), BF),
            pltpu.VMEM((TRUNC, HALF), BF),
            pltpu.VMEM((TRUNC, HALF), BF),
            pltpu.VMEM((MR, KP), F32),
            pltpu.VMEM((CH, FIELDS, MR, QUART), BF),
            pltpu.VMEM((CH, FIELDS, MR, QUART), BF),
            pltpu.VMEM((RW * FIELDS * LEV, FIELDS * MR), BF),
            pltpu.VMEM((2, RW, FIELDS * LEV, QUART), BF),
            pltpu.SemaphoreType.DMA((SLOTS,)),
            pltpu.SemaphoreType.DMA((2,)),
            pltpu.SemaphoreType.DMA,
            pltpu.SemaphoreType.DMA((len(PIECES),)),
            pltpu.SemaphoreType.DMA,
            pltpu.SemaphoreType.DMA((CH,)),
            pltpu.SemaphoreType.DMA((2, RW)),
        ],
        compiler_params=pltpu.CompilerParams(collective_id=0, has_side_effects=True, vmem_limit_bytes=60 << 20),
        name="transform",
    )(wave_slot, spectra, legendre, block_mask, slots, lats, levels, jnp.asarray(key_rows()), jnp.asarray(basis_table()))


def solution(mesh):
    placed = (
        P("wave", None, "field", None),
        P("wave", None, None),
        P("wave", None, None),
        P(),
        P(),
        P(),
    )
    return jax.shard_map(
        shards, mesh=mesh, in_specs=placed, out_specs=P("wave", None, "field"), check_vma=False
    )
```

time: 458 us -> 99.7 us (0.22); the launches traced: 450 us -> 99.4 us
  local copies, waits for them, and re-layouts: 247 us -> 4.96 us
  other arithmetic: 98.1 us -> 3.84 us
  Pallas kernels: 0 us -> 90.6 us
  waiting for transfers between devices: 56.3 us -> 0 us
  matrix products: 29.8 us -> 0 us
  starting transfers between devices: 18.8 us -> 0 us
    unnamed x15 -> x1, local copies, waits for them, and re-layouts: 105 us -> 4.96 us
    pallas_call x0 -> x1, Pallas kernels: none -> 90.6 us  [shards(): pl.pallas_call(transform_kernel, out_shape=jax.ShapeDtypeStruct((ROWS, FI...]
    dot_general x2 -> x0, other arithmetic: 72.8 us -> none  [the longest x1 36.7 us: synthesize(): jnp.einsum('stcl,scq->tlq', coeff_rows, low_part, preferred_element_type=...]
    gather x2 -> x0, local copies, waits for them, and re-layouts: 58.1 us -> none  [the longest x1 46.7 us: shards(): coeffs = jnp.take(coeffs, lat_order, axis=1)]
    all_to_all x2 -> x0, waiting for transfers between devices: 56.3 us -> none  [the longest x1 56.3 us: shards(): lax.all_to_all(grid_local, 'field', split_axis=2, concat_axis=1, tiled=True)]
    all_to_all x4 -> x0, local copies, waits for them, and re-layouts: 47.3 us -> none  [the longest x2 28.6 us: shards(): lax.all_to_all(grid_local, 'field', split_axis=2, concat_axis=1, tiled=True)]
    dot_general x4 -> x0, matrix products: 29.8 us -> none  [the longest x1 11.4 us: synthesize(): jnp.einsum('stcl,scq->tlq', coeff_rows, high_part, preferred_element_type...]
    convert_element_type x1 -> x0, local copies, waits for them, and re-layouts: 19.3 us -> none  [synthesize(): return (from_high + from_low).astype(jnp.bfloat16)]
  transfers between devices with their start and end apart: 2 -> 0, of which waited for: 1 -> 0; matrix products, arithmetic and copies ran while one was open for 16% -> 0% of each run, Pallas kernels for 0% -> 0%
where the time goes in v2:
time: 99.7 us; the launch traced here: 99.4 us
  Pallas kernels  90.6 us (91%)
  local copies, waits for them, and re-layouts  4.96 us (5%)
  other arithmetic  3.84 us (4%)
    pallas_call x1, Pallas kernels, shards(): pl.pallas_call(transform_kernel, out_shape=jax.ShapeDtypeStruct((ROWS, FI...  90.6 us
    unnamed x1, local copies, waits for them, and re-layouts  4.96 us

profile of v2, /device:TPU:1, one launch (start us, length us, event | category | flops | bytes accessed | tf_op | source)
XLA Modules:
  0.0 99.4 jit_solution(6778763029067576915)
XLA Ops:
  0.0 1.3 %convert_bitcast_fusion.2.levels_ref = f32[2,128]{1,0:T(2,128)} fusion(s32[160]{0:T(256)} %param.13), kind=kLoop, calls=%fused_computation.2 | loop fusion | flops 256 | bytes 1664 | tf_op jit(solution)/shard_map/reshape | solution.py:307
  1.3 1.3 %convert_bitcast_fusion.1.slots_ref = f32[5,128]{1,0:T(8,128)} fusion(s32[640]{0:T(1024)} %ws_ref.1), kind=kLoop, calls=%fused_computation.1 | loop fusion | flops 640 | bytes 5120 | tf_op jit(solution)/shard_map/reshape | solution.py:305
  2.6 1.3 %convert_bitcast_fusion.lats_ref = f32[10,128]{1,0:T(8,128)} fusion(s32[1280]{0:T(1024)} %param.12), kind=kLoop, calls=%fused_computation | loop fusion | flops 1280 | bytes 10240 | tf_op jit(solution)/shard_map/reshape | solution.py:306
  3.8 90.6 %transform.1 = bf16[20,160,768]{2,1,0:T(8,128)(2,1)} custom-call(s32[640]{0:T(1024)} %ws_ref.1, bf16[10,2,40,640]{3,2,1,0:T(8,128)(2,1)} %spec_ref.1, bf16[10,640,640]{2,1,0:T(8,128)(2,1)} %leg_ref.1, s32[10,10,10]{2,1,0:T(8,128)} %mask_ref.1, f32[5,128]{1,0:T(8,128)} %convert_bitcast_fusion.1.slots_ref, f32[10,128]{1,0:T(8,128)} %convert_bitcast_fusion.lats_ref, ...), custom_call_target="tpu_custom_call" | custom-call | tf_op jit(solution)/shard_map/transform/pallas_call | solution.py:310
  94.5 5.0 %copy.10 = bf16[20,160,768]{2,1,0:T(8,128)(2,1)} copy(bf16[20,160,768]{2,1,0:T(8,128)(2,1)} %transform.1) | data formatting | bytes 9830400

commit v3 on v2

--- a/solution.py
+++ b/solution.py
@@ -36,12 +36,12 @@
 MR = RW * LEV
 CUT = 3
 LT = NLAT // 128
-PIECES = [(0, 0, CUT), (0, CUT, NG)] + [(c, 0, NG) for c in range(1, CH)]
+PIECES = [(0, CUT), (CUT, NG)]
 
 
 def row_runs():
     runs, at = [], 0
-    for low, high in ((0, CUT), (CUT, NG)):
+    for low, high in PIECES:
         for k in range(KG):
             top = min(high, (LEV - k + KG - 1) // KG)
             runs.append((k, low, top, at))
@@ -79,6 +79,7 @@
 
 
 def columns_of(rows):
+    rows = rows.astype(F32)
     return jnp.concatenate([column_of(rows[t : t + 1, :]) for t in range(rows.shape[0])], axis=0)
 
 
@@ -178,8 +179,12 @@
     return first, last - first
 
 
-def fill_levels(levels, colkey, pick):
-    col = columns_of(levels[...])[: FIELDS * LEV]
+def fill_levels(levels, column, colkey, pick):
+    @pl.loop(0, FIELDS * LEV)
+    def _(k):
+        column[pl.ds(k, 1), :] = jnp.full((1, 128), levels[k].astype(F32), F32)
+
+    col = column[: FIELDS * LEV, :]
     for i in range(RW):
         for j in range(FIELDS * MR // 128):
             hit = col + float(1000 * i) == colkey[1:2, j * 128 : (j + 1) * 128]
@@ -220,34 +225,33 @@
         legendre_slot(s, ws_ref[SLOTS * w + s], spec, leg, mask_ref, kept, z)
 
     zb[...] = jnp.concatenate([z[t] for t in range(LT)], axis=1).astype(BF)
-
+    pl.semaphore_wait(barrier, WAVES + FIELDS - 2)
     my_tile, my_place = w // TW, lax.rem(w, TW)
 
-    def wave_copy(p, peer):
-        c, low, high = PIECES[p]
+    def wave_copy(c, p, peer):
+        span = pl.ds(PIECES[p][0], PIECES[p][1] - PIECES[p][0])
         return pltpu.make_async_remote_copy(
-            src_ref=send.at[c, peer, pl.ds(low, high - low)],
-            dst_ref=recv.at[c, my_tile, my_place, pl.ds(low, high - low)],
+            src_ref=send.at[c, peer, span],
+            dst_ref=recv.at[c, my_tile, my_place, span],
             send_sem=send_sem,
-            recv_sem=recv_sem.at[p],
+            recv_sem=recv_sem.at[c, p],
             device_id=(peer, f),
             device_id_type=MESH,
         )
 
-    for p, (c, low, high) in enumerate(PIECES):
-        if low == 0:
-            pack_chunk(c, vcol, oht, zb, send)
-        if p == 0:
-            pl.semaphore_wait(barrier, WAVES + FIELDS - 2)
-        span = pl.ds(low, high - low)
-        pltpu.make_async_copy(send.at[c, w, span], recv.at[c, my_tile, my_place, span], recv_sem.at[p]).start()
-
-        @pl.loop(1, WAVES // 2)
-        def _(d):
-            wave_copy(p, lax.rem(w + d, WAVES)).start()
-            wave_copy(p, lax.rem(w + WAVES - d, WAVES)).start()
-
-        wave_copy(p, lax.rem(w + WAVES // 2, WAVES)).start()
+    @pl.loop(0, CH)
+    def _(c):
+        pack_chunk(c, vcol, oht, zb, send)
+        for p, (low, high) in enumerate(PIECES):
+            span = pl.ds(low, high - low)
+            pltpu.make_async_copy(send.at[c, w, span], recv.at[c, my_tile, my_place, span], recv_sem.at[c, p]).start()
+
+            @pl.loop(1, WAVES // 2)
+            def _(d):
+                wave_copy(c, p, lax.rem(w + d, WAVES)).start()
+                wave_copy(c, p, lax.rem(w + WAVES - d, WAVES)).start()
+
+            wave_copy(c, p, lax.rem(w + WAVES // 2, WAVES)).start()
 
     for c in range(CH):
         for j in range(WAVES - TW * (NT - 1), TW):
@@ -256,44 +260,52 @@
     fill_order(slots_ref, keycol, perm)
     loads[1].wait()
     fill_tables(basis, t_even, t_odd)
-    fill_levels(levels_ref, keys_ref, pick)
+    fill_levels(levels_ref, keycol, keys_ref, pick)
 
     def out_copies(c):
-        return [pltpu.make_async_copy(stage.at[c % 2, i], out_ref.at[CH * i + c], out_sem.at[c % 2, i]) for i in range(RW)]
+        slot = lax.rem(c, 2)
+        return [pltpu.make_async_copy(stage.at[slot, i], out_ref.at[CH * i + c], out_sem.at[slot, i]) for i in range(RW)]
 
     def finish_chunk(c):
         pltpu.make_async_copy(xrecv.at[c], xrecv.at[c], xrecv_sem.at[c]).wait()
         rows = xrecv[c].reshape(FIELDS * MR, QUART)
-        if c >= 2:
+
+        @pl.when(c >= 2)
+        def _():
             for copy in out_copies(c - 2):
                 copy.wait()
+
         values = jnp.dot(pick[...], rows, preferred_element_type=F32).astype(BF)
-        stage[c % 2] = values.reshape(RW, FIELDS * LEV, QUART)
+        stage[lax.rem(c, 2)] = values.reshape(RW, FIELDS * LEV, QUART)
         for copy in out_copies(c):
             copy.start()
 
-    for p, (c, low, high) in enumerate(PIECES):
-        landed = send.at[c, :, pl.ds(low, high - low)]
-        pltpu.make_async_copy(landed, landed, recv_sem.at[p]).wait()
-        first, count = fourier_piece(c, low, high, recv, regroup, lhs, perm, t_even, t_odd, quarters)
-        part = pl.ds(first, count)
-        pltpu.make_async_copy(quarters.at[c, f, part], xrecv.at[c, f, part], xrecv_sem.at[c]).start()
-        for d in range(1, FIELDS):
-            peer = lax.rem(f + d, FIELDS)
-            pltpu.make_async_remote_copy(
-                src_ref=quarters.at[c, peer, part],
-                dst_ref=xrecv.at[c, f, part],
-                send_sem=xsend_sem,
-                recv_sem=xrecv_sem.at[c],
-                device_id=(w, peer),
-                device_id_type=MESH,
-            ).start()
-        if high == NG and c >= 1:
+    @pl.loop(0, CH)
+    def _(c):
+        for p, (low, high) in enumerate(PIECES):
+            landed = send.at[c, :, pl.ds(low, high - low)]
+            pltpu.make_async_copy(landed, landed, recv_sem.at[c, p]).wait()
+            first, count = fourier_piece(c, low, high, recv, regroup, lhs, perm, t_even, t_odd, quarters)
+            part = pl.ds(first, count)
+            pltpu.make_async_copy(quarters.at[c, f, part], xrecv.at[c, f, part], xrecv_sem.at[c]).start()
+            for d in (1, 3, 2):
+                peer = lax.rem(f + d, FIELDS)
+                pltpu.make_async_remote_copy(
+                    src_ref=quarters.at[c, peer, part],
+                    dst_ref=xrecv.at[c, f, part],
+                    send_sem=xsend_sem,
+                    recv_sem=xrecv_sem.at[c],
+                    device_id=(w, peer),
+                    device_id_type=MESH,
+                ).start()
+
+        @pl.when(c >= 1)
+        def _():
             finish_chunk(c - 1)
-    finish_chunk(CH - 1)
-
+
+    finish_chunk(jnp.int32(CH - 1))
     for c in (CH - 2, CH - 1):
-        for copy in out_copies(c):
+        for copy in out_copies(jnp.int32(c)):
             copy.wait()
     sent = quarters.at[:, pl.ds(0, FIELDS - 1)]
     pltpu.make_async_copy(sent, sent, xsend_sem).wait()
@@ -302,15 +314,15 @@
 
 
 def shards(spectra, legendre, block_mask, wave_slot, lat_order, level_order):
-    slots = wave_slot.astype(F32).reshape(TRUNC // 128, 128)
-    lats = lat_order.astype(F32).reshape(LT, 128)
-    levels = jnp.pad(level_order, (0, 256 - FIELDS * LEV)).astype(F32).reshape(2, 128)
+    slots = wave_slot.reshape(TRUNC // 128, 128)
+    lats = lat_order.reshape(LT, 128)
     anyspace = pl.BlockSpec(memory_space=pl.ANY)
     vmem = pl.BlockSpec(memory_space=pltpu.VMEM)
+    smem = pl.BlockSpec(memory_space=pltpu.SMEM)
     return pl.pallas_call(
         transform_kernel,
         out_shape=jax.ShapeDtypeStruct((ROWS, FIELDS * LEV, QUART), BF),
-        in_specs=[pl.BlockSpec(memory_space=pltpu.SMEM), anyspace, anyspace, vmem, vmem, vmem, vmem, vmem, anyspace],
+        in_specs=[smem, anyspace, anyspace, vmem, vmem, vmem, smem, vmem, anyspace],
         out_specs=anyspace,
         scratch_shapes=[
             pltpu.VMEM((SLOTS, 2, LEV, TRUNC), BF),
@@ -336,14 +348,14 @@
             pltpu.SemaphoreType.DMA((SLOTS,)),
             pltpu.SemaphoreType.DMA((2,)),
             pltpu.SemaphoreType.DMA,
-            pltpu.SemaphoreType.DMA((len(PIECES),)),
+            pltpu.SemaphoreType.DMA((CH, len(PIECES))),
             pltpu.SemaphoreType.DMA,
             pltpu.SemaphoreType.DMA((CH,)),
             pltpu.SemaphoreType.DMA((2, RW)),
         ],
         compiler_params=pltpu.CompilerParams(collective_id=0, has_side_effects=True, vmem_limit_bytes=60 << 20),
         name="transform",
-    )(wave_slot, spectra, legendre, block_mask, slots, lats, levels, jnp.asarray(key_rows()), jnp.asarray(basis_table()))
+    )(wave_slot, spectra, legendre, block_mask, slots, lats, level_order, jnp.asarray(key_rows()), jnp.asarray(basis_table()))
 
 
 def solution(mesh):

time: 99.7 us -> 91.8 us (0.921)
  Pallas kernels: 90.6 us -> 86.6 us
  other arithmetic: 3.84 us -> 0 us
    pallas_call x1, Pallas kernels: 90.6 us -> 86.6 us  [shards(): pl.pallas_call(transform_kernel, out_shape=jax.ShapeDtypeStruct((ROWS, FI...]
    reshape x3 -> x0, other arithmetic: 3.84 us -> none  [the longest x1 1.3 us: shards(): lats = lat_order.astype(F32).reshape(LT, 128)]
where the time goes in v3:
time: 91.8 us; the launch traced here: 91.6 us
  Pallas kernels  86.6 us (94%)
  local copies, waits for them, and re-layouts  4.96 us (5%)
    pallas_call x1, Pallas kernels, shards(): pl.pallas_call(transform_kernel, out_shape=jax.ShapeDtypeStruct((ROWS, FI...  86.6 us
    unnamed x1, local copies, waits for them, and re-layouts  4.96 us

profile of v3, /device:TPU:1, one launch (start us, length us, event | category | flops | bytes accessed | tf_op | source)
XLA Modules:
  0.0 91.6 jit_solution(3763970465407439538)
XLA Ops:
  0.0 86.6 %transform.1 = bf16[20,160,768]{2,1,0:T(8,128)(2,1)} custom-call(s32[640]{0:T(1024)} %ws_ref.1, bf16[10,2,40,640]{3,2,1,0:T(8,128)(2,1)} %spec_ref.1, bf16[10,640,640]{2,1,0:T(8,128)(2,1)} %leg_ref.1, s32[10,10,10]{2,1,0:T(8,128)} %mask_ref.1, s32[5,128]{1,0:T(8,128)} %bitcast.2, s32[10,128]{1,0:T(8,128)} %bitcast.3, s32[160]{0:T(256)} %levels_ref.1, ...), custom_call_target="tpu_custom_call" | custom-call | tf_op jit(solution)/shard_map/transform/pallas_call | solution.py:322
  86.6 5.0 %copy.10 = bf16[20,160,768]{2,1,0:T(8,128)(2,1)} copy(bf16[20,160,768]{2,1,0:T(8,128)(2,1)} %transform.1) | data formatting | bytes 9830400

commit v4 on v3

--- a/solution.py
+++ b/solution.py
@@ -36,6 +36,7 @@
 MR = RW * LEV
 CUT = 3
 LT = NLAT // 128
+GREET = 7
 PIECES = [(0, CUT), (CUT, NG)]
 
 
@@ -194,8 +195,8 @@
 def transform_kernel(
     ws_ref, spec_ref, leg_ref, mask_ref, slots_ref, lats_ref, levels_ref, keys_ref, basis_ref, out_ref,
     spec, leg, kept, z, zb, vcol, oht, send, recv, basis, regroup, keycol, perm, t_even, t_odd, lhs,
-    quarters, xrecv, pick, stage,
-    leg_sem, load_sem, send_sem, recv_sem, xsend_sem, xrecv_sem, out_sem,
+    quarters, xrecv, pick,
+    leg_sem, load_sem, send_sem, recv_sem, xsend_sem, xrecv_sem,
 ):
     w, f = lax.axis_index("wave"), lax.axis_index("field")
     loads = [pltpu.make_async_copy(spec_ref, spec, load_sem.at[0]), pltpu.make_async_copy(basis_ref, basis, load_sem.at[1])]
@@ -206,11 +207,6 @@
     loads[1].start()
 
     barrier = pltpu.get_barrier_semaphore()
-
-    @pl.loop(1, WAVES)
-    def _(d):
-        pl.semaphore_signal(barrier, inc=1, device_id=(lax.rem(w + d, WAVES), f), device_id_type=MESH)
-
     for d in range(1, FIELDS):
         pl.semaphore_signal(barrier, inc=1, device_id=(w, lax.rem(f + d, FIELDS)), device_id_type=MESH)
 
@@ -221,6 +217,12 @@
 
     @pl.loop(0, SLOTS)
     def _(s):
+        @pl.when(s < (WAVES - 1) // GREET)
+        def _():
+            for t in range(GREET):
+                peer = lax.rem(w + GREET * s + t + 1, WAVES)
+                pl.semaphore_signal(barrier, inc=1, device_id=(peer, f), device_id_type=MESH)
+
         pltpu.make_async_copy(leg_ref.at[s], leg.at[s], leg_sem.at[s]).wait()
         legendre_slot(s, ws_ref[SLOTS * w + s], spec, leg, mask_ref, kept, z)
 
@@ -239,8 +241,7 @@
             device_id_type=MESH,
         )
 
-    @pl.loop(0, CH)
-    def _(c):
+    def send_chunk(c):
         pack_chunk(c, vcol, oht, zb, send)
         for p, (low, high) in enumerate(PIECES):
             span = pl.ds(low, high - low)
@@ -253,6 +254,7 @@
 
             wave_copy(c, p, lax.rem(w + WAVES // 2, WAVES)).start()
 
+    send_chunk(0)
     for c in range(CH):
         for j in range(WAVES - TW * (NT - 1), TW):
             recv[c, NT - 1, j] = jnp.zeros((NG, RW, 128), BF)
@@ -260,25 +262,15 @@
     fill_order(slots_ref, keycol, perm)
     loads[1].wait()
     fill_tables(basis, t_even, t_odd)
+    send_chunk(1)
     fill_levels(levels_ref, keycol, keys_ref, pick)
-
-    def out_copies(c):
-        slot = lax.rem(c, 2)
-        return [pltpu.make_async_copy(stage.at[slot, i], out_ref.at[CH * i + c], out_sem.at[slot, i]) for i in range(RW)]
 
     def finish_chunk(c):
         pltpu.make_async_copy(xrecv.at[c], xrecv.at[c], xrecv_sem.at[c]).wait()
         rows = xrecv[c].reshape(FIELDS * MR, QUART)
-
-        @pl.when(c >= 2)
-        def _():
-            for copy in out_copies(c - 2):
-                copy.wait()
-
         values = jnp.dot(pick[...], rows, preferred_element_type=F32).astype(BF)
-        stage[lax.rem(c, 2)] = values.reshape(RW, FIELDS * LEV, QUART)
-        for copy in out_copies(c):
-            copy.start()
+        for i in range(RW):
+            out_ref[CH * i + c] = values[FIELDS * LEV * i : FIELDS * LEV * (i + 1), :]
 
     @pl.loop(0, CH)
     def _(c):
@@ -299,14 +291,15 @@
                     device_id_type=MESH,
                 ).start()
 
+        @pl.when(c + 2 < CH)
+        def _():
+            send_chunk(c + 2)
+
         @pl.when(c >= 1)
         def _():
             finish_chunk(c - 1)
 
-    finish_chunk(jnp.int32(CH - 1))
-    for c in (CH - 2, CH - 1):
-        for copy in out_copies(jnp.int32(c)):
-            copy.wait()
+    finish_chunk(CH - 1)
     sent = quarters.at[:, pl.ds(0, FIELDS - 1)]
     pltpu.make_async_copy(sent, sent, xsend_sem).wait()
     left = send.at[:, pl.ds(0, WAVES - 1)]
@@ -321,9 +314,9 @@
     smem = pl.BlockSpec(memory_space=pltpu.SMEM)
     return pl.pallas_call(
         transform_kernel,
-        out_shape=jax.ShapeDtypeStruct((ROWS, FIELDS * LEV, QUART), BF),
+        out_shape=pltpu.VMEM((ROWS, FIELDS * LEV, QUART), BF),
         in_specs=[smem, anyspace, anyspace, vmem, vmem, vmem, smem, vmem, anyspace],
-        out_specs=anyspace,
+        out_specs=vmem,
         scratch_shapes=[
             pltpu.VMEM((SLOTS, 2, LEV, TRUNC), BF),
             pltpu.VMEM((SLOTS, TRUNC, TRUNC), BF),
@@ -344,16 +337,14 @@
             pltpu.VMEM((CH, FIELDS, MR, QUART), BF),
             pltpu.VMEM((CH, FIELDS, MR, QUART), BF),
             pltpu.VMEM((RW * FIELDS * LEV, FIELDS * MR), BF),
-            pltpu.VMEM((2, RW, FIELDS * LEV, QUART), BF),
             pltpu.SemaphoreType.DMA((SLOTS,)),
             pltpu.SemaphoreType.DMA((2,)),
             pltpu.SemaphoreType.DMA,
             pltpu.SemaphoreType.DMA((CH, len(PIECES))),
             pltpu.SemaphoreType.DMA,
             pltpu.SemaphoreType.DMA((CH,)),
-            pltpu.SemaphoreType.DMA((2, RW)),
         ],
-        compiler_params=pltpu.CompilerParams(collective_id=0, has_side_effects=True, vmem_limit_bytes=60 << 20),
+        compiler_params=pltpu.CompilerParams(collective_id=0, has_side_effects=True, vmem_limit_bytes=57 << 20),
         name="transform",
     )(wave_slot, spectra, legendre, block_mask, slots, lats, level_order, jnp.asarray(key_rows()), jnp.asarray(basis_table()))
 

time: 91.8 us -> 89.2 us (0.972)
  local copies, waits for them, and re-layouts: 4.96 us -> 2.25 us
    unnamed x1, local copies, waits for them, and re-layouts: 4.96 us -> 2.25 us
where the time goes in v4:
time: 89.2 us; the launch traced here: 89.1 us
  Pallas kernels  86.8 us (97%)
  local copies, waits for them, and re-layouts  2.25 us (3%)
    pallas_call x1, Pallas kernels, shards(): pl.pallas_call(transform_kernel, out_shape=pltpu.VMEM((ROWS, FIELDS * LEV...  86.8 us
    unnamed x1, local copies, waits for them, and re-layouts  2.25 us

profile of v4, /device:TPU:1, one launch (start us, length us, event | category | flops | bytes accessed | tf_op | source)
XLA Modules:
  0.0 89.1 jit_solution(17136757663513114551)
XLA Ops:
  0.0 86.8 %transform.1 = bf16[20,160,768]{2,1,0:T(8,128)(2,1)S(1)} custom-call(s32[640]{0:T(1024)} %ws_ref.1, bf16[10,2,40,640]{3,2,1,0:T(8,128)(2,1)} %spec_ref.1, bf16[10,640,640]{2,1,0:T(8,128)(2,1)} %leg_ref.1, s32[10,10,10]{2,1,0:T(8,128)} %mask_ref.1, s32[5,128]{1,0:T(8,128)} %bitcast.2, s32[10,128]{1,0:T(8,128)} %bitcast.3, s32[160]{0:T(256)} %levels_ref.1, ...), custom_call_target="tpu_custom_call" | custom-call | tf_op jit(solution)/shard_map/transform/pallas_call | solution.py:315
  86.8 2.3 %copy.10 = bf16[20,160,768]{2,1,0:T(8,128)(2,1)} copy(bf16[20,160,768]{2,1,0:T(8,128)(2,1)S(1)} %transform.1) | data formatting | bytes 9830400

commit v5 on v4

--- a/solution.py
+++ b/solution.py
@@ -36,7 +36,7 @@
 MR = RW * LEV
 CUT = 3
 LT = NLAT // 128
-GREET = 7
+GREET = 21
 PIECES = [(0, CUT), (CUT, NG)]
 
 
@@ -123,11 +123,18 @@
                 z[t + TRUNC // 128, dst, :] = south[src, t * 128 : (t + 1) * 128]
 
 
-def pack_chunk(c, vcol, oht, zb, send):
-    fill_onehot(oht, vcol[pl.ds(c, NLAT // CH, stride=CH), :], NLAT)
-    rows = lax.dot_general(oht[...], zb[...], (((1,), (1,)), ((), ())), preferred_element_type=F32)
-    for g in range(NG):
-        send[c, :, g] = rows[:, 128 * g : 128 * (g + 1)].reshape(WAVES, RW, 128).astype(BF)
+def round_piece(low, high, z, zb):
+    part = slice(128 * low, 128 * high)
+    for t in range(LT):
+        zb[part, 128 * t : 128 * (t + 1)] = z[t, part, :].astype(BF)
+
+
+def pack_piece(c, low, high, oht, zb, send):
+    rows = lax.dot_general(
+        oht[...], zb[128 * low : 128 * high, :], (((1,), (1,)), ((), ())), preferred_element_type=F32
+    )
+    for g in range(low, high):
+        send[c, :, g] = rows[:, 128 * (g - low) : 128 * (g - low + 1)].reshape(WAVES, RW, 128).astype(BF)
 
 
 def fill_order(slots, keycol, perm):
@@ -213,21 +220,28 @@
     lat = columns_of(lats_ref[...])
     vcol[...] = jnp.where(lat < TRUNC, lat, (NLAT + TRUNC - 1) - lat)
     clear_pads(z)
+
+    def choose_rows(c):
+        fill_onehot(oht, vcol[pl.ds(c, NLAT // CH, stride=CH), :], NLAT)
+
+    choose_rows(0)
     loads[0].wait()
 
-    @pl.loop(0, SLOTS)
-    def _(s):
-        @pl.when(s < (WAVES - 1) // GREET)
+    @pl.loop(0, SLOTS // 2)
+    def _(pair):
+        @pl.when(pair < (WAVES - 1) // GREET)
         def _():
             for t in range(GREET):
-                peer = lax.rem(w + GREET * s + t + 1, WAVES)
+                peer = lax.rem(w + GREET * pair + t + 1, WAVES)
                 pl.semaphore_signal(barrier, inc=1, device_id=(peer, f), device_id_type=MESH)
 
-        pltpu.make_async_copy(leg_ref.at[s], leg.at[s], leg_sem.at[s]).wait()
-        legendre_slot(s, ws_ref[SLOTS * w + s], spec, leg, mask_ref, kept, z)
-
-    zb[...] = jnp.concatenate([z[t] for t in range(LT)], axis=1).astype(BF)
-    pl.semaphore_wait(barrier, WAVES + FIELDS - 2)
+        for half in range(2):
+            s = 2 * pair + half
+            pltpu.make_async_copy(leg_ref.at[s], leg.at[s], leg_sem.at[s]).wait()
+        for half in range(2):
+            s = 2 * pair + half
+            legendre_slot(s, ws_ref[SLOTS * w + s], spec, leg, mask_ref, kept.at[half], z)
+
     my_tile, my_place = w // TW, lax.rem(w, TW)
 
     def wave_copy(c, p, peer):
@@ -241,24 +255,33 @@
             device_id_type=MESH,
         )
 
+    def send_piece(c, p):
+        low, high = PIECES[p]
+        span = pl.ds(low, high - low)
+        pack_piece(c, low, high, oht, zb, send)
+        pltpu.make_async_copy(send.at[c, w, span], recv.at[c, my_tile, my_place, span], recv_sem.at[c, p]).start()
+
+        @pl.loop(1, WAVES // 2)
+        def _(d):
+            wave_copy(c, p, lax.rem(w + d, WAVES)).start()
+            wave_copy(c, p, lax.rem(w + WAVES - d, WAVES)).start()
+
+        wave_copy(c, p, lax.rem(w + WAVES // 2, WAVES)).start()
+
     def send_chunk(c):
-        pack_chunk(c, vcol, oht, zb, send)
-        for p, (low, high) in enumerate(PIECES):
-            span = pl.ds(low, high - low)
-            pltpu.make_async_copy(send.at[c, w, span], recv.at[c, my_tile, my_place, span], recv_sem.at[c, p]).start()
-
-            @pl.loop(1, WAVES // 2)
-            def _(d):
-                wave_copy(c, p, lax.rem(w + d, WAVES)).start()
-                wave_copy(c, p, lax.rem(w + WAVES - d, WAVES)).start()
-
-            wave_copy(c, p, lax.rem(w + WAVES // 2, WAVES)).start()
-
-    send_chunk(0)
+        choose_rows(c)
+        for p in range(len(PIECES)):
+            send_piece(c, p)
+
+    round_piece(*PIECES[0], z, zb)
+    pl.semaphore_wait(barrier, WAVES + FIELDS - 2)
+    send_piece(0, 0)
+    round_piece(*PIECES[1], z, zb)
+    fill_onehot(regroup, column_of(keys_ref[0:1, :]), KG * 128)
+    send_piece(0, 1)
     for c in range(CH):
         for j in range(WAVES - TW * (NT - 1), TW):
             recv[c, NT - 1, j] = jnp.zeros((NG, RW, 128), BF)
-    fill_onehot(regroup, column_of(keys_ref[0:1, :]), KG * 128)
     fill_order(slots_ref, keycol, perm)
     loads[1].wait()
     fill_tables(basis, t_even, t_odd)
@@ -320,7 +343,7 @@
         scratch_shapes=[
             pltpu.VMEM((SLOTS, 2, LEV, TRUNC), BF),
             pltpu.VMEM((SLOTS, TRUNC, TRUNC), BF),
-            pltpu.VMEM((TRUNC, TRUNC), BF),
+            pltpu.VMEM((2, TRUNC, TRUNC), BF),
             pltpu.VMEM((LT, NG * 128, 128), F32),
             pltpu.VMEM((NG * 128, NLAT), BF),
             pltpu.VMEM((NLAT, 128), F32),

time: 89.2 us -> 86.9 us (0.974)
  Pallas kernels: 86.8 us -> 84.4 us
    pallas_call x1, Pallas kernels: 86.8 us -> 84.4 us  [shards(): pl.pallas_call(transform_kernel, out_shape=pltpu.VMEM((ROWS, FIELDS * LEV...]
where the time goes in v5:
time: 86.9 us; the launch traced here: 86.6 us
  Pallas kernels  84.4 us (97%)
  local copies, waits for them, and re-layouts  2.25 us (3%)
    pallas_call x1, Pallas kernels, shards(): pl.pallas_call(transform_kernel, out_shape=pltpu.VMEM((ROWS, FIELDS * LEV...  84.4 us
    unnamed x1, local copies, waits for them, and re-layouts  2.25 us

profile of v5, /device:TPU:1, one launch (start us, length us, event | category | flops | bytes accessed | tf_op | source)
XLA Modules:
  0.0 86.6 jit_solution(12244857794912130200)
XLA Ops:
  0.0 84.4 %transform.1 = bf16[20,160,768]{2,1,0:T(8,128)(2,1)S(1)} custom-call(s32[640]{0:T(1024)} %ws_ref.1, bf16[10,2,40,640]{3,2,1,0:T(8,128)(2,1)} %spec_ref.1, bf16[10,640,640]{2,1,0:T(8,128)(2,1)} %leg_ref.1, s32[10,10,10]{2,1,0:T(8,128)} %mask_ref.1, s32[5,128]{1,0:T(8,128)} %bitcast.2, s32[10,128]{1,0:T(8,128)} %bitcast.3, s32[160]{0:T(256)} %levels_ref.1, ...), custom_call_target="tpu_custom_call" | custom-call | tf_op jit(solution)/shard_map/transform/pallas_call | solution.py:338
  84.4 2.3 %copy.10 = bf16[20,160,768]{2,1,0:T(8,128)(2,1)} copy(bf16[20,160,768]{2,1,0:T(8,128)(2,1)S(1)} %transform.1) | data formatting | bytes 9830400

commit v6 on v5

--- a/solution.py
+++ b/solution.py
@@ -97,30 +97,36 @@
     z[:, first : 128 * NG, :] = jnp.zeros((LT, 128 * NG - first, 128), F32)
 
 
-def legendre_slot(s, wavenum, spec, leg, mask, kept, z):
+def mask_slot(s, leg, mask):
     jb = lax.broadcasted_iota(jnp.int32, (NB, TRUNC), 0) * BLOCK
     jj = lax.broadcasted_iota(jnp.int32, (NB, TRUNC), 1)
     widen = ((jj >= jb) & (jj < jb + BLOCK)).astype(F32)
     lanes = jnp.dot((mask[s] > 0).astype(F32), widen, preferred_element_type=F32).astype(BF)
     for b in range(NB):
-        kept[b * BLOCK : (b + 1) * BLOCK, :] = leg[s, b * BLOCK : (b + 1) * BLOCK, :] * lanes[b : b + 1, :]
+        leg[s, b * BLOCK : (b + 1) * BLOCK, :] = leg[s, b * BLOCK : (b + 1) * BLOCK, :] * lanes[b : b + 1, :]
+
+
+def legendre_piece(s, wavenum, low, high, spec, leg, z):
+    first = KG * low // 8 * 8
+    last = min(LEV, -(-KG * high // 8) * 8)
+    n_rows = last - first
     degree = lax.broadcasted_iota(jnp.int32, (1, TRUNC), 1)
     upper = degree >= wavenum
     even = ((degree + wavenum) & 1) == 0
-    rows = spec[s].reshape(2 * LEV, TRUNC)
+    rows = jnp.concatenate([spec[s, comp, first:last, :] for comp in range(2)], axis=0)
     rows_e = rows * jnp.where(upper & even, 1.0, 0.0).astype(BF)
     rows_o = rows * jnp.where(upper & ~even, 1.0, 0.0).astype(BF)
-    both = jnp.dot(jnp.concatenate([rows_e, rows_o], axis=0), kept[...], preferred_element_type=F32)
-    sums_e, sums_o = both[: 2 * LEV], both[2 * LEV :]
+    both = jnp.dot(jnp.concatenate([rows_e, rows_o], axis=0), leg[s], preferred_element_type=F32)
+    sums_e, sums_o = both[: 2 * n_rows], both[2 * n_rows :]
     north, south = sums_e + sums_o, sums_e - sums_o
     for comp in range(2):
-        for g in range(NG):
+        for g in range(low, high):
             n = min(KG, LEV - KG * g)
-            src = slice(LEV * comp + KG * g, LEV * comp + KG * g + n)
+            at = n_rows * comp + KG * g - first
             dst = pl.ds(128 * g + SLOTS * comp + s, n, stride=SC)
             for t in range(TRUNC // 128):
-                z[t, dst, :] = north[src, t * 128 : (t + 1) * 128]
-                z[t + TRUNC // 128, dst, :] = south[src, t * 128 : (t + 1) * 128]
+                z[t, dst, :] = north[at : at + n, t * 128 : (t + 1) * 128]
+                z[t + TRUNC // 128, dst, :] = south[at : at + n, t * 128 : (t + 1) * 128]
 
 
 def round_piece(low, high, z, zb):
@@ -201,7 +207,7 @@
 
 def transform_kernel(
     ws_ref, spec_ref, leg_ref, mask_ref, slots_ref, lats_ref, levels_ref, keys_ref, basis_ref, out_ref,
-    spec, leg, kept, z, zb, vcol, oht, send, recv, basis, regroup, keycol, perm, t_even, t_odd, lhs,
+    spec, leg, z, zb, vcol, oht, send, recv, basis, regroup, keycol, perm, t_even, t_odd, lhs,
     quarters, xrecv, pick,
     leg_sem, load_sem, send_sem, recv_sem, xsend_sem, xrecv_sem,
 ):
@@ -240,7 +246,8 @@
             pltpu.make_async_copy(leg_ref.at[s], leg.at[s], leg_sem.at[s]).wait()
         for half in range(2):
             s = 2 * pair + half
-            legendre_slot(s, ws_ref[SLOTS * w + s], spec, leg, mask_ref, kept.at[half], z)
+            mask_slot(s, leg, mask_ref)
+            legendre_piece(s, ws_ref[SLOTS * w + s], *PIECES[0], spec, leg, z)
 
     my_tile, my_place = w // TW, lax.rem(w, TW)
 
@@ -276,6 +283,13 @@
     round_piece(*PIECES[0], z, zb)
     pl.semaphore_wait(barrier, WAVES + FIELDS - 2)
     send_piece(0, 0)
+
+    @pl.loop(0, SLOTS // 2)
+    def _(pair):
+        for half in range(2):
+            s = 2 * pair + half
+            legendre_piece(s, ws_ref[SLOTS * w + s], *PIECES[1], spec, leg, z)
+
     round_piece(*PIECES[1], z, zb)
     fill_onehot(regroup, column_of(keys_ref[0:1, :]), KG * 128)
     send_piece(0, 1)
@@ -343,7 +357,6 @@
         scratch_shapes=[
             pltpu.VMEM((SLOTS, 2, LEV, TRUNC), BF),
             pltpu.VMEM((SLOTS, TRUNC, TRUNC), BF),
-            pltpu.VMEM((2, TRUNC, TRUNC), BF),
             pltpu.VMEM((LT, NG * 128, 128), F32),
             pltpu.VMEM((NG * 128, NLAT), BF),
             pltpu.VMEM((NLAT, 128), F32),

time: 86.9 us -> 88.1 us (1.014)
  Pallas kernels: 84.4 us -> 85.8 us
    pallas_call x1, Pallas kernels: 84.4 us -> 85.8 us  [shards(): pl.pallas_call(transform_kernel, out_shape=pltpu.VMEM((ROWS, FIELDS * LEV...]
where the time goes in v6:
time: 88.1 us; the launch traced here: 88 us
  Pallas kernels  85.8 us (97%)
  local copies, waits for them, and re-layouts  2.25 us (3%)
    pallas_call x1, Pallas kernels, shards(): pl.pallas_call(transform_kernel, out_shape=pltpu.VMEM((ROWS, FIELDS * LEV...  85.8 us
    unnamed x1, local copies, waits for them, and re-layouts  2.25 us

profile of v6, /device:TPU:1, one launch (start us, length us, event | category | flops | bytes accessed | tf_op | source)
XLA Modules:
  0.0 88.0 jit_solution(3263535299395064974)
XLA Ops:
  0.0 85.8 %transform.1 = bf16[20,160,768]{2,1,0:T(8,128)(2,1)S(1)} custom-call(s32[640]{0:T(1024)} %ws_ref.1, bf16[10,2,40,640]{3,2,1,0:T(8,128)(2,1)} %spec_ref.1, bf16[10,640,640]{2,1,0:T(8,128)(2,1)} %leg_ref.1, s32[10,10,10]{2,1,0:T(8,128)} %mask_ref.1, s32[5,128]{1,0:T(8,128)} %bitcast.2, s32[10,128]{1,0:T(8,128)} %bitcast.3, s32[160]{0:T(256)} %levels_ref.1, ...), custom_call_target="tpu_custom_call" | custom-call | tf_op jit(solution)/shard_map/transform/pallas_call | solution.py:352
  85.8 2.3 %copy.10 = bf16[20,160,768]{2,1,0:T(8,128)(2,1)} copy(bf16[20,160,768]{2,1,0:T(8,128)(2,1)S(1)} %transform.1) | data formatting | bytes 9830400

commit v7 on v5

--- a/solution.py
+++ b/solution.py
@@ -162,7 +162,7 @@
     t_odd[n:, QUART:] = (basis[2 * n : 3 * n, :].astype(F32) * -sign).astype(BF)
 
 
-def fourier_piece(c, low, high, recv, regroup, lhs, perm, t_even, t_odd, quarters):
+def fourier_piece(c, low, high, recv, regroup, lhs, perm, t_even, t_odd, quarters, deliver):
     ng = high - low
     blocks = jnp.concatenate(
         [recv[c, :, j, low:high].reshape(NT * ng * RW, 128) for j in range(TW)], axis=1
@@ -184,7 +184,8 @@
         g_odd = jnp.dot(ordered[:, TRUNC:], t_odd[:, cols], preferred_element_type=F32)
         quarters[c, h, first:last, :] = (g_even + g_odd).astype(BF)
         quarters[c, h + 2, first:last, :] = (g_even - g_odd).astype(BF)
-    return first, last - first
+        for q in (h, h + 2):
+            deliver(q, pl.ds(first, last - first))
 
 
 def fill_levels(levels, column, colkey, pick):
@@ -285,8 +286,6 @@
     fill_order(slots_ref, keycol, perm)
     loads[1].wait()
     fill_tables(basis, t_even, t_odd)
-    send_chunk(1)
-    fill_levels(levels_ref, keycol, keys_ref, pick)
 
     def finish_chunk(c):
         pltpu.make_async_copy(xrecv.at[c], xrecv.at[c], xrecv_sem.at[c]).wait()
@@ -297,26 +296,39 @@
 
     @pl.loop(0, CH)
     def _(c):
+        def deliver(q, part):
+            @pl.when(f == q)
+            def _():
+                pltpu.make_async_copy(quarters.at[c, q, part], xrecv.at[c, q, part], xrecv_sem.at[c]).start()
+
+            @pl.when(f != q)
+            def _():
+                pltpu.make_async_remote_copy(
+                    src_ref=quarters.at[c, q, part],
+                    dst_ref=xrecv.at[c, f, part],
+                    send_sem=xsend_sem,
+                    recv_sem=xrecv_sem.at[c],
+                    device_id=(w, q),
+                    device_id_type=MESH,
+                ).start()
+
         for p, (low, high) in enumerate(PIECES):
             landed = send.at[c, :, pl.ds(low, high - low)]
             pltpu.make_async_copy(landed, landed, recv_sem.at[c, p]).wait()
-            first, count = fourier_piece(c, low, high, recv, regroup, lhs, perm, t_even, t_odd, quarters)
-            part = pl.ds(first, count)
-            pltpu.make_async_copy(quarters.at[c, f, part], xrecv.at[c, f, part], xrecv_sem.at[c]).start()
-            for d in (1, 3, 2):
-                peer = lax.rem(f + d, FIELDS)
-                pltpu.make_async_remote_copy(
-                    src_ref=quarters.at[c, peer, part],
-                    dst_ref=xrecv.at[c, f, part],
-                    send_sem=xsend_sem,
-                    recv_sem=xrecv_sem.at[c],
-                    device_id=(w, peer),
-                    device_id_type=MESH,
-                ).start()
+            fourier_piece(c, low, high, recv, regroup, lhs, perm, t_even, t_odd, quarters, deliver)
+            if p == 0:
+
+                @pl.when(c == 0)
+                def _():
+                    send_chunk(1)
 
         @pl.when(c + 2 < CH)
         def _():
             send_chunk(c + 2)
+
+        @pl.when(c == 0)
+        def _():
+            fill_levels(levels_ref, keycol, keys_ref, pick)
 
         @pl.when(c >= 1)
         def _():

time: 86.9 us -> 88.8 us (1.022)
  Pallas kernels: 84.4 us -> 86.4 us
    pallas_call x1, Pallas kernels: 84.4 us -> 86.4 us  [shards(): pl.pallas_call(transform_kernel, out_shape=pltpu.VMEM((ROWS, FIELDS * LEV...]
where the time goes in v7:
time: 88.8 us; the launch traced here: 88.7 us
  Pallas kernels  86.4 us (97%)
  local copies, waits for them, and re-layouts  2.25 us (3%)
    pallas_call x1, Pallas kernels, shards(): pl.pallas_call(transform_kernel, out_shape=pltpu.VMEM((ROWS, FIELDS * LEV...  86.4 us
    unnamed x1, local copies, waits for them, and re-layouts  2.25 us

profile of v7, /device:TPU:1, one launch (start us, length us, event | category | flops | bytes accessed | tf_op | source)
XLA Modules:
  0.0 88.7 jit_solution(9159644617928577155)
XLA Ops:
  0.0 86.4 %transform.1 = bf16[20,160,768]{2,1,0:T(8,128)(2,1)S(1)} custom-call(s32[640]{0:T(1024)} %ws_ref.1, bf16[10,2,40,640]{3,2,1,0:T(8,128)(2,1)} %spec_ref.1, bf16[10,640,640]{2,1,0:T(8,128)(2,1)} %leg_ref.1, s32[10,10,10]{2,1,0:T(8,128)} %mask_ref.1, s32[5,128]{1,0:T(8,128)} %bitcast.2, s32[10,128]{1,0:T(8,128)} %bitcast.3, s32[160]{0:T(256)} %levels_ref.1, ...), custom_call_target="tpu_custom_call" | custom-call | tf_op jit(solution)/shard_map/transform/pallas_call | solution.py:350
  86.4 2.3 %copy.10 = bf16[20,160,768]{2,1,0:T(8,128)(2,1)} copy(bf16[20,160,768]{2,1,0:T(8,128)(2,1)S(1)} %transform.1) | data formatting | bytes 9830400

commit v8 on v5

--- a/solution.py
+++ b/solution.py
@@ -286,7 +286,6 @@
     loads[1].wait()
     fill_tables(basis, t_even, t_odd)
     send_chunk(1)
-    fill_levels(levels_ref, keycol, keys_ref, pick)
 
     def finish_chunk(c):
         pltpu.make_async_copy(xrecv.at[c], xrecv.at[c], xrecv_sem.at[c]).wait()
@@ -317,6 +316,10 @@
         @pl.when(c + 2 < CH)
         def _():
             send_chunk(c + 2)
+
+        @pl.when(c == 0)
+        def _():
+            fill_levels(levels_ref, keycol, keys_ref, pick)
 
         @pl.when(c >= 1)
         def _():

time: 86.9 us -> 87 us (level)
  no operation moved by 1% of the time
where the time goes in v8:
time: 87 us; the launch traced here: 86.9 us
  Pallas kernels  84.6 us (97%)
  local copies, waits for them, and re-layouts  2.25 us (3%)
    pallas_call x1, Pallas kernels, shards(): pl.pallas_call(transform_kernel, out_shape=pltpu.VMEM((ROWS, FIELDS * LEV...  84.6 us
    unnamed x1, local copies, waits for them, and re-layouts  2.25 us

profile of v8, /device:TPU:1, one launch (start us, length us, event | category | flops | bytes accessed | tf_op | source)
XLA Modules:
  0.0 86.9 jit_solution(5315535011880057716)
XLA Ops:
  0.0 84.6 %transform.1 = bf16[20,160,768]{2,1,0:T(8,128)(2,1)S(1)} custom-call(s32[640]{0:T(1024)} %ws_ref.1, bf16[10,2,40,640]{3,2,1,0:T(8,128)(2,1)} %spec_ref.1, bf16[10,640,640]{2,1,0:T(8,128)(2,1)} %leg_ref.1, s32[10,10,10]{2,1,0:T(8,128)} %mask_ref.1, s32[5,128]{1,0:T(8,128)} %bitcast.2, s32[10,128]{1,0:T(8,128)} %bitcast.3, s32[160]{0:T(256)} %levels_ref.1, ...), custom_call_target="tpu_custom_call" | custom-call | tf_op jit(solution)/shard_map/transform/pallas_call | solution.py:341
  84.7 2.3 %copy.10 = bf16[20,160,768]{2,1,0:T(8,128)(2,1)} copy(bf16[20,160,768]{2,1,0:T(8,128)(2,1)S(1)} %transform.1) | data formatting | bytes 9830400
